TPU v7x, 128 devices: a whole 4x4x4 slice. The times are simulated.
128 devices in a mesh: dom: 16 (over x, y), cls: 8 (over z, core).
Axes of the slice: x: 4, y: 4, z: 4, core: 2. Of those that a mesh axis runs over, the one named last changes fastest.
Arguments:
- stack: bfloat16 [32768, 2, 64, 128], P(('dom', 'cls')), may hold values from -6 to 6
- batch_index: int32 [16384], P(('dom', 'cls')), may hold values from 0 to 255, as said below
- best_class: int32 [16384], P(('dom', 'cls')), may hold values from 0 to 511, as said below
- best_rot: int32 [16384], P(('dom', 'cls')), may hold values from 0 to 63
- best_shift: int32 [16384, 2], P(('dom', 'cls')), may hold values from -4 to 4
- ctf: bfloat16 [16384, 64], P(('dom', 'cls')), may hold values from -1 to 1
- averages: float32 [512, 2, 64, 128], P(('dom', 'cls')), may hold values from -6 to 6
- velocity: float32 [512, 2, 64, 128], P(('dom', 'cls')), may hold values from -3 to 3
Outputs:
- new_averages: float32 [512, 2, 64, 128], P(('dom', 'cls'))
- new_velocity: float32 [512, 2, 64, 128], P(('dom', 'cls'))
- errors: float32 [16384], P(('dom', 'cls'))
Inputs may be any that keep to these rules, and one draw needn't show every extreme that they name: `batch_index`: each aligned block of 128 entries (one device's particles) holds distinct row numbers into that device's own 256 rows of stack. `best_class`: classes c with equal c // 32 form a group. In each aligned block of 128 entries (one device's particles) at most 16 entries name classes of one group, and some group is named by exactly 16 entries of that block.
All inputs are finite; a program needn't handle non-finite values.
Results may differ from a plain program's by a relative error of at most 0.0026.
Values may be sent and summed in bfloat16 or wider, within the bound.
No kernel may reach another device: no remote copies, remote signals or barrier semaphores. Data moves between devices by JAX's collectives and lax.ppermute only.
A program may use at most 128 MiB of HBM per device.

v0:
```python
import jax
import jax.numpy as jnp
from jax import lax
from jax.sharding import PartitionSpec as P

IMG = 128


TWO_PI = 6.283185307179586
MOMENTUM = 0.9
RATE = 0.5
RIDGE = 1.0


def align_rows(rows, rotation, shift):
    cycles = rows.shape[2]
    angles = rows.shape[3]
    radius = jnp.arange(cycles).astype(jnp.float32) + 1.0
    theta = TWO_PI * jnp.arange(angles).astype(jnp.float32) / angles
    shift_x = shift[:, 0].astype(jnp.float32)
    shift_y = shift[:, 1].astype(jnp.float32)
    along = (
        jnp.cos(theta)[None, None, :] * shift_x[:, None, None]
        + jnp.sin(theta)[None, None, :] * shift_y[:, None, None]
    )
    phase = TWO_PI * radius[None, :, None] * along / IMG
    cosine = jnp.cos(phase)
    sine = jnp.sin(phase)
    real = rows[:, 0].astype(jnp.float32)
    imag = rows[:, 1].astype(jnp.float32)
    turned = jnp.stack([cosine * real - sine * imag, sine * real + cosine * imag], axis=1).astype(
        jnp.bfloat16
    )
    source = (jnp.arange(angles)[None, :] + 2 * rotation[:, None]) % angles
    permute = (source[:, :, None] == jnp.arange(angles)[None, None, :]).astype(jnp.bfloat16)
    moved = jnp.einsum("pskb,pab->pska", turned, permute, preferred_element_type=jnp.float32)
    return moved.astype(jnp.bfloat16)


def class_table(marker, column):
    local = marker.astype(jnp.int32) - 1
    return (jnp.arange(column)[:, None] == local[None, :]).astype(jnp.bfloat16)


def class_partials(table, terms, gamma):
    grads = jnp.dot(table, terms, preferred_element_type=jnp.float32)
    gamma_float = gamma.astype(jnp.float32)
    weights = jnp.dot(
        table.astype(jnp.float32),
        gamma_float * gamma_float,
        precision=lax.Precision.HIGHEST,
        preferred_element_type=jnp.float32,
    )
    return (grads, weights)


def on_device(stack, batch_index, best_class, best_rot, best_shift, ctf, averages, velocity):
    count = batch_index.shape[0]
    cycles = ctf.shape[1]
    angles = stack.shape[3]
    stored = stack.shape[0]
    flat = 2 * cycles * angles
    owners = lax.axis_size("dom")
    column = lax.axis_size("cls") * averages.shape[0]
    slots = 2 * count // owners
    buffer_rows = owners * slots
    picker = (batch_index[:, None] == jnp.arange(stored)[None, :]).astype(jnp.bfloat16)
    rows = jnp.dot(picker, stack.reshape(stored, flat), preferred_element_type=jnp.float32)
    rows = rows.astype(jnp.bfloat16).reshape(count, 2, cycles, angles)
    aligned = align_rows(rows, best_rot, best_shift)
    owner = best_class // column
    local_class = best_class - owner * column
    placed = (owner[:, None] == jnp.arange(owners)[None, :]).astype(jnp.int32)
    position = jnp.sum(jnp.cumsum(placed, axis=0) * placed, axis=1) - 1
    target = owner * slots + position
    dispatch = (jnp.arange(buffer_rows)[:, None] == target[None, :]).astype(jnp.bfloat16)

    def pack(payload):
        packed = jnp.dot(dispatch, payload, preferred_element_type=jnp.float32).astype(jnp.bfloat16)
        return packed.reshape(owners, slots, payload.shape[1])

    ctf_packed = pack(ctf)
    marker_packed = pack((local_class + 1).astype(jnp.bfloat16)[:, None]).reshape(owners, slots)
    every = lax.all_gather(averages.astype(jnp.bfloat16), ("dom", "cls"), axis=0, tiled=True)
    total_classes = every.shape[0]
    chooser = (best_class[:, None] == jnp.arange(total_classes)[None, :]).astype(jnp.bfloat16)
    model = jnp.dot(
        chooser, every.reshape(total_classes, flat), preferred_element_type=jnp.float32
    ).reshape(count, 2, cycles, angles)
    gamma_wide = ctf.astype(jnp.float32)[:, None, :, None]
    resid = aligned.astype(jnp.float32) - gamma_wide * model
    errors = jnp.mean(resid * resid, axis=(1, 2, 3))
    term = (gamma_wide * resid).astype(jnp.bfloat16).reshape(count, flat)
    arrived = (
        lax.all_to_all(pack(term), "dom", split_axis=0, concat_axis=0, tiled=True),
        lax.all_to_all(ctf_packed, "dom", split_axis=0, concat_axis=0, tiled=True),
        lax.all_to_all(marker_packed, "dom", split_axis=0, concat_axis=0, tiled=True),
    )
    got_terms = arrived[0].reshape(buffer_rows, flat)
    got_gamma = arrived[1].reshape(buffer_rows, cycles)
    table = class_table(arrived[2].reshape(buffer_rows), column)
    grads, weights = class_partials(table, got_terms, got_gamma)
    summed, weight_sum = (
        lax.psum_scatter(grads, "cls", scatter_dimension=0, tiled=True),
        lax.psum_scatter(weights, "cls", scatter_dimension=0, tiled=True),
    )
    step = (summed.reshape(averages.shape) - RIDGE * averages) / (
        weight_sum[:, None, :, None] + RIDGE
    )
    new_velocity = MOMENTUM * velocity + step
    new_averages = averages + RATE * new_velocity
    return (new_averages, new_velocity, errors)


def solution(mesh):
    in_specs = (
        P(("dom", "cls"), None, None, None),
        P(("dom", "cls")),
        P(("dom", "cls")),
        P(("dom", "cls")),
        P(("dom", "cls"), None),
        P(("dom", "cls"), None),
        P(("dom", "cls"), None, None, None),
        P(("dom", "cls"), None, None, None),
    )
    out_specs = (
        P(("dom", "cls"), None, None, None),
        P(("dom", "cls"), None, None, None),
        P(("dom", "cls")),
    )
    return jax.shard_map(
        on_device, mesh=mesh, in_specs=in_specs, out_specs=out_specs, check_vma=False
    )
```

profile of v0, /device:TPU:1, one launch (start us, length us, event | category | flops | bytes accessed | tf_op | source)
XLA Modules:
  0.0 394.8 jit_solution(6878493428379385242)
XLA Ops:
  7.2 1.6 convert_element_type.118
  8.9 0.7 and_select_fusion
  9.6 0.2 reduce_window_sum.11
  9.8 0.2 select_reduce_fusion
  10.0 0.7 add_add_fusion
  10.6 0.8 fusion.30
  11.4 0.7 all_to_all.16
  12.2 7.6 %all-to-all-start = ((bf16[16,1,16]{2,1,0:T(2,128)(2,1)}), bf16[16,1,16]{2,1,0:T(2,128)(2,1)S(1)}, u32[]{:S(2)}, u32[]{:S(2)}) async-start(bf16[16,1,16]{2,1,0:T(2,128)(2,1)} %all_to_all.16), calls=%async_computation | async-start | bytes 16384 | tf_op jit(solution)/shard_map/all_to_all | solution.py:97
  19.7 0.8 copy.19
  20.6 8.8 %fusion.24 = bf16[16,8,128,128]{3,1,2,0:T(8,128)(2,1)S(1)} fusion(bf16[32,8,128,128]{3,2,1,0:T(8,128)(2,1)} %bitcast.59, s32[128]{0:T(128)} %param.9), kind=kOutput, calls=%fused_computation.30 | convolution fusion | flops 1075871744 | bytes 12583424 | tf_op jit(solution)/shard_map/dot_general | solution.py:68
  29.4 1.2 copy.27
  31.0 17.4 %fusion.8 = (bf16[128,1,64,128]{3,2,1,0:T(8,128)(2,1)S(1)}, bf16[128,1,64,128]{3,2,1,0:T(8,128)(2,1)}) fusion(f32[128,128]{1,0:T(8,128)S(1)} %multiply_add_fusion.1, f32[64]{0:T(128)S(1)} %add_multiply_fusion, bf16[128,2,64,128]{3,2,1,0:T(8,128)(2,1)S(1)} %bitcast.58), kind=kLoop, calls=%fused_computation.17 | loop fusion | flops 12582912 | bytes 8454400 | tf_op jit(solution)/shard_map/convert
  48.4 47.4 %all-gather.2.cloned.1.call-done = bf16[512,2,64,128]{3,2,1,0:T(8,128)(2,1)} async-done(((bf16[4,2,64,128]{3,2,1,0:T(8,128)(2,1)}), bf16[512,2,64,128]{3,2,1,0:T(8,128)(2,1)}) %all-gather.2.cloned.1.call-update) | async-done | bytes 16777232 | tf_op jit(solution)/shard_map/all_gather | solution.py:84
  95.8 23.9 %copy.25 = bf16[512,2,64,128]{0,3,2,1:T(8,128)(2,1)} copy(bf16[512,2,64,128]{3,2,1,0:T(8,128)(2,1)} %all-gather.2.cloned.1.call-done) | data formatting | bytes 33554432 | tf_op jit(solution)/shard_map/reshape | solution.py:88
  119.7 13.6 %fusion = f32[128,2,64,128]{0,3,2,1:T(8,128)} fusion(bf16[512,2,64,128]{0,3,2,1:T(8,128)(2,1)} %copy.25, s32[128]{0:T(128)S(1)} %copy-done.4), kind=kOutput, calls=%fused_computation.2 | convolution fusion | flops 2147549184 | bytes 25166336 | tf_op jit(solution)/shard_map/dot_general | solution.py:87
  133.3 8.7 %copy.21 = f32[128,2,64,128]{3,2,1,0:T(8,128)} copy(f32[128,2,64,128]{0,3,2,1:T(8,128)} %fusion) | data formatting | bytes 16777216 | tf_op jit(solution)/shard_map/dot_general | solution.py:87
  142.0 9.4 %multiply_reduce_fusion = (f32[128]{0:T(128)S(1)}, bf16[128,2,64,128]{3,2,1,0:T(8,128)(2,1)S(1)}) fusion(f32[128,2,64,128]{3,2,1,0:T(8,128)} %copy.21, f32[128,64]{1,0:T(8,128)S(1)} %copy.19, s32[128,128]{1,0:T(8,128)S(1)} %add_select_fusion, bf16[128,1,64,128]{3,2,1,0:T(8,128)(2,1)} %get-tuple-element.8, bf16[128,1,64,128]{3,2,1,0:T(8,128)(2,1)S(1)} %get-tuple-element.7), kind=kOutput, calls=%fused_computation.6 | convolution fusion | flops 557842304 | bytes 16876032 | tf_op jit(solution)/shard_map/pskb,pab->pska/dot_general | solution.py:36
  151.4 6.7 %convolution_convert_fusion = bf16[256,16384]{1,0:T(8,128)(2,1)} fusion(bf16[16,8,128,128]{3,2,1,0:T(8,128)(2,1)S(1)} %bitcast.60, s32[128]{0:T(128)S(1)} %add_add_fusion), kind=kOutput, calls=%fused_computation | convolution fusion | flops 1077968896 | bytes 12583424 | tf_op jit(solution)/shard_map/dot_general | solution.py:79
  158.1 6.6 %all-to-all-start.1 = ((bf16[16,16,16384]{2,1,0:T(8,128)(2,1)}), bf16[16,16,16384]{2,1,0:T(8,128)(2,1)}, u32[]{:S(2)}, u32[]{:S(2)}) async-start(bf16[16,16,16384]{2,1,0:T(8,128)(2,1)} %bitcast.57), calls=%async_computation.1 | async-start | bytes 16777216 | tf_op jit(solution)/shard_map/all_to_all | solution.py:95
  164.8 145.6 %all-to-all-done.1 = bf16[16,16,16384]{2,1,0:T(8,128)(2,1)} async-done(((bf16[16,16,16384]{2,1,0:T(8,128)(2,1)}), bf16[16,16,16384]{2,1,0:T(8,128)(2,1)}, u32[]{:S(2)}, u32[]{:S(2)}) %all-to-all-start.1) | async-done | bytes 8388640 | tf_op jit(solution)/shard_map/all_to_all | solution.py:95
  310.4 6.3 %fusion.41 = f32[32,16384]{1,0:T(8,128)} fusion(bf16[256,16384]{1,0:T(8,128)(2,1)} %bitcast.12, s32[256]{0:T(256)S(1)} %sub.32), kind=kOutput, calls=%fused_computation.59 | convolution fusion | flops 268443648 | bytes 10486784 | tf_op jit(solution)/shard_map/dot_general | solution.py:46
  316.7 0.1 convolution_convert_fusion.2
  317.0 0.7 reshape.217
  317.7 10.8 %all-to-all-start.2 = ((bf16[16,2,512]{2,1,0:T(2,128)(2,1)}), bf16[16,2,512]{2,1,0:T(2,128)(2,1)S(1)}, u32[]{:S(2)}, u32[]{:S(2)}) async-start(bf16[16,2,512]{2,1,0:T(2,128)(2,1)} %reshape.217), calls=%async_computation.2 | async-start | bytes 65536 | tf_op jit(solution)/shard_map/all_to_all | solution.py:96
  328.6 0.6 dynamic-slice
  329.8 5.2 %all-to-all-done.2 = bf16[16,2,512]{2,1,0:T(2,128)(2,1)S(1)} async-done(((bf16[16,2,512]{2,1,0:T(2,128)(2,1)}), bf16[16,2,512]{2,1,0:T(2,128)(2,1)S(1)}, u32[]{:S(2)}, u32[]{:S(2)}) %all-to-all-start.2) | async-done | bytes 32800 | tf_op jit(solution)/shard_map/all_to_all | solution.py:96
  335.2 0.2 fusion.40
  335.4 23.1 %all-reduce.1 = f32[32,64]{1,0:T(8,128)S(1)} all-reduce(f32[32,64]{1,0:T(8,128)S(1)} %fusion.40), channel_id=3, replica_groups=mesh['dom'=16,'cls'=8] {'cls'}, use_global_device_ids=true, to_apply=%region_3.4.clone | all-reduce | flops 2048 | bytes 16384
  358.5 0.5 broadcast_multiply_fusion
  359.0 26.9 %all-reduce.4.cloned.1.call-done = f32[32,16384]{1,0:T(8,128)} async-done(((f32[32,16384]{1,0:T(8,128)}), f32[32,16384]{1,0:T(8,128)}) %all-reduce.4.cloned.1.call-update) | async-done | bytes 2097168
  385.9 1.1 dynamic-slice_bitcast_fusion
  387.0 1.0 multiply_add_fusion
  (34 shorter events, 0.9 us)
Async XLA Ops:
  7.2 88.6 %all-gather.2.cloned.1.call-start = ((), (), s32[]{:S(2)}) async-start(), calls=%async_computation.3 | async-start | bytes 16908288 | tf_op jit(solution)/shard_map/all_gather | solution.py:84
  12.2 145.9 %all-to-all-start = ((bf16[16,1,16]{2,1,0:T(2,128)(2,1)}), bf16[16,1,16]{2,1,0:T(2,128)(2,1)S(1)}, u32[]{:S(2)}, u32[]{:S(2)}) async-start(bf16[16,1,16]{2,1,0:T(2,128)(2,1)} %all_to_all.16), calls=%async_computation | async-start | bytes 16384 | tf_op jit(solution)/shard_map/all_to_all | solution.py:97
  29.4 1.3 copy-start.5
  29.4 1.3 copy-start.3
  48.4 71.4 %copy-start.4 = (s32[128]{0:T(128)S(1)}, s32[128]{0:T(128)}, u32[]{:S(2)}) copy-start(s32[128]{0:T(128)} %param.10) | copy-start | bytes 1540
  158.1 152.3 %all-to-all-start.1 = ((bf16[16,16,16384]{2,1,0:T(8,128)(2,1)}), bf16[16,16,16384]{2,1,0:T(8,128)(2,1)}, u32[]{:S(2)}, u32[]{:S(2)}) async-start(bf16[16,16,16384]{2,1,0:T(8,128)(2,1)} %bitcast.57), calls=%async_computation.1 | async-start | bytes 16777216 | tf_op jit(solution)/shard_map/all_to_all | solution.py:95
  164.7 221.2 %all-reduce.4.cloned.1.call-start = ((), (), s32[]{:S(2)}) async-start(), calls=%async_computation.4 | async-start | bytes 4194304
  310.4 6.3 %copy-start.2 = (bf16[128,64]{0,1:T(8,128)(2,1)S(1)}, bf16[128,64]{0,1:T(8,128)(2,1)}, u32[]{:S(2)}) copy-start(bf16[128,64]{0,1:T(8,128)(2,1)} %param.13) | copy-start | bytes 49156
  310.4 18.2 %copy-start.6 = (u32[128]{0:T(128)S(1)}, u32[128]{0:T(128)}, u32[]{:S(2)}) copy-start(u32[128]{0:T(128)} %constant.71) | copy-start | bytes 1540
  310.4 76.6 %copy-start = (f32[4,2,64,128]{3,2,1,0:T(8,128)S(1)}, f32[4,2,64,128]{3,2,1,0:T(8,128)}, u32[]{:S(2)}) copy-start(f32[4,2,64,128]{3,2,1,0:T(8,128)} %param.14) | copy-start | bytes 786436
  310.4 76.6 %copy-start.1 = (f32[4,2,64,128]{3,2,1,0:T(8,128)S(1)}, f32[4,2,64,128]{3,2,1,0:T(8,128)}, u32[]{:S(2)}) copy-start(f32[4,2,64,128]{3,2,1,0:T(8,128)} %param.15) | copy-start | bytes 786436
  317.7 17.3 %all-to-all-start.2 = ((bf16[16,2,512]{2,1,0:T(2,128)(2,1)}), bf16[16,2,512]{2,1,0:T(2,128)(2,1)S(1)}, u32[]{:S(2)}, u32[]{:S(2)}) async-start(bf16[16,2,512]{2,1,0:T(2,128)(2,1)} %reshape.217), calls=%async_computation.2 | async-start | bytes 65536 | tf_op jit(solution)/shard_map/all_to_all | solution.py:96
Sparse Core Ops, SparseCore 0:
  11.7 83.9 all-gather.1
  316.8 68.9 all-reduce.3
where the time goes:
time: 397 us; the launch traced here: 395 us
  waiting for transfers between devices  225 us (57%)
  matrix products  45.9 us (12%)
  local copies, waits for them, and re-layouts  38.1 us (10%)
  starting transfers between devices  25.1 us (6%)
  blocking collectives  23.1 us (6%)
  other arithmetic  22.6 us (6%)
  between operations  14.9 us (4%)
    all_to_all x1, waiting for transfers between devices, on_device(): lax.all_to_all(pack(term), 'dom', split_axis=0, concat_axis=0, tiled=True)  146 us
    all_gather x1, waiting for transfers between devices, on_device(): lax.all_gather(averages.astype(jnp.bfloat16), ('dom', 'cls'), axis=0, til...  47.4 us
    unnamed x3, waiting for transfers between devices  26.9 us
    reshape x1, local copies, waits for them, and re-layouts, on_device(): every.reshape(total_classes, flat)  23.9 us
    unnamed x1, blocking collectives  23.1 us
    another operation x1, other arithmetic  17.4 us
    dot_general x1, matrix products, on_device(): jnp.dot(chooser, every.reshape(total_classes, flat), preferred_element_ty...  13.6 us
    all_to_all x1, starting transfers between devices, on_device(): lax.all_to_all(ctf_packed, 'dom', split_axis=0, concat_axis=0, tiled=True)  10.8 us
  transfers between devices with their start and end apart: 5, of which 4 were waited for; matrix products, arithmetic and copies ran while one was open for 24% of the time, Pallas kernels for 0%

commit v1 on v0

v1 whole, which is shorter than its diff:
```python
import numpy as np
import jax
import jax.numpy as jnp
from jax import lax
from jax.experimental import pallas as pl
from jax.experimental.pallas import tpu as pltpu
from jax.sharding import PartitionSpec as P

IMG = 128
TOP_SHIFT = 4
MOMENTUM = 0.9
RATE = 0.5
RIDGE = 1.0
BATCH = 16
SOURCES = 16
AUX = 8
HALF_CLASSES = 256


def phase_tables(cycles, angles):
    radius = np.arange(1, cycles + 1, dtype=np.float64)[:, None]
    theta = 2.0 * np.pi * np.arange(angles, dtype=np.float64)[None, :] / angles
    shifts = np.arange(-TOP_SHIFT, TOP_SHIFT + 1, dtype=np.float64)[:, None, None]
    tables = []
    for along in (np.cos(theta), np.sin(theta)):
        phase = 2.0 * np.pi * radius * along / IMG * shifts
        tables.append(np.stack([np.cos(phase), np.sin(phase)], axis=1))
    return np.stack(tables).astype(np.float32)


def align_kernel(index_ref, rot_ref, shift_ref, *refs):
    blocks = refs[:BATCH]
    table_ref, ctf_ref, class_ref, averages_ref, out_ref, turned_ref = refs[BATCH:]
    step = pl.program_id(0)
    cycles, angles = table_ref.shape[3], table_ref.shape[4]
    grid_rows = 2 * cycles
    count = ctf_ref.shape[0]
    for j in range(BATCH):
        particle = step * BATCH + j
        sx = shift_ref[0, particle] + TOP_SHIFT
        sy = shift_ref[1, particle] + TOP_SHIFT
        back = (angles - 2 * rot_ref[particle]) % angles
        xr, xi = table_ref[0, sx, 0], table_ref[0, sx, 1]
        yr, yi = table_ref[1, sy, 0], table_ref[1, sy, 1]
        cosine = xr * yr - xi * yi
        sine = xr * yi + xi * yr
        real = blocks[j][0, 0].astype(jnp.float32)
        imag = blocks[j][0, 1].astype(jnp.float32)
        base = j * grid_rows
        turned_ref[base : base + cycles, :] = pltpu.roll(cosine * real - sine * imag, back, 1)
        turned_ref[base + cycles : base + grid_rows, :] = pltpu.roll(
            sine * real + cosine * imag, back, 1
        )
    first = pl.multiple_of(step * BATCH, BATCH)

    def spread(r, carry):
        got = turned_ref[pl.ds(r, BATCH, stride=grid_rows), :]
        out_ref[r, pl.ds(first, BATCH), :] = got.astype(jnp.bfloat16)
        return carry

    lax.fori_loop(0, grid_rows, spread, 0, unroll=16)

    @pl.when(step == pl.num_programs(0) - 1)
    def _():
        classes = (class_ref[...] - HALF_CLASSES).astype(jnp.float32)
        turned_ref[0:grid_rows, :] = jnp.broadcast_to(classes, (grid_rows, angles))
        gamma = ctf_ref[...].astype(jnp.float32).T
        turned_ref[grid_rows : grid_rows + cycles, :] = gamma
        turned_ref[grid_rows + cycles : 2 * grid_rows, :] = gamma
        owned = averages_ref.shape[0]
        for j in range(owned):
            turned_ref[(2 + j) * grid_rows : (3 + j) * grid_rows, :] = averages_ref[j]
        for j in range(2 + owned, AUX):
            turned_ref[j * grid_rows : (j + 1) * grid_rows, :] = jnp.zeros(
                (grid_rows, angles), jnp.float32
            )

        def spread_aux(r, carry):
            got = turned_ref[pl.ds(r, AUX, stride=grid_rows), :]
            out_ref[r, pl.ds(count, AUX), :] = got.astype(jnp.bfloat16)
            return carry

        lax.fori_loop(0, grid_rows, spread_aux, 0, unroll=16)


def align(stack, batch_index, best_class, best_rot, best_shift, ctf, averages):
    count = batch_index.shape[0]
    cycles, angles = stack.shape[2], stack.shape[3]
    grid_rows = 2 * cycles
    owned = averages.shape[0]

    def pick(j):
        return pl.BlockSpec(
            (1, 2, cycles, angles), lambda i, index, rot, shift: (index[i * BATCH + j], 0, 0, 0)
        )

    def whole(shape):
        return pl.BlockSpec(shape, lambda i, index, rot, shift: (0,) * len(shape))

    table = jnp.asarray(phase_tables(cycles, angles))
    return pl.pallas_call(
        align_kernel,
        out_shape=jax.ShapeDtypeStruct((grid_rows, count + AUX, angles), jnp.bfloat16),
        grid_spec=pltpu.PrefetchScalarGridSpec(
            num_scalar_prefetch=3,
            grid=(count // BATCH,),
            in_specs=[pick(j) for j in range(BATCH)]
            + [
                whole(table.shape),
                whole((count, cycles)),
                whole((1, count)),
                whole((owned, grid_rows, angles)),
            ],
            out_specs=whole((grid_rows, count + AUX, angles)),
            scratch_shapes=[pltpu.VMEM((BATCH * grid_rows, angles), jnp.float32)],
        ),
        compiler_params=pltpu.CompilerParams(
            dimension_semantics=("arbitrary",), vmem_limit_bytes=48 << 20
        ),
        name="align",
    )(
        batch_index,
        best_rot,
        best_shift.T,
        *([stack] * BATCH),
        table,
        ctf,
        best_class.reshape(1, count),
        averages.reshape(owned, grid_rows, angles),
    )


def classes_kernel(
    rows_ref,
    aux_ref,
    out_ref,
    aux32_ref,
    class_ref,
    gamma_ref,
    model_ref,
    sums_ref,
    grads_ref,
    weights_ref,
    error_ref,
):
    step = pl.program_id(0)
    devices, angles = aux_ref.shape[0], aux_ref.shape[2]
    count = rows_ref.shape[1]
    classes = model_ref.shape[0]
    owned = classes // devices

    @pl.when(step == 0)
    def _():
        aux32_ref[...] = aux_ref[...].astype(jnp.float32).reshape(devices * AUX, angles)
        class_ref[...] = aux32_ref[pl.ds(0, devices, stride=AUX), :]
        gamma_ref[...] = aux32_ref[pl.ds(1, devices, stride=AUX), :]
        for j in range(owned):
            grads_ref[pl.ds(j, devices, stride=owned), :] = aux32_ref[
                pl.ds(2 + j, devices, stride=AUX), :
            ]
        model_ref[...] = grads_ref[...].astype(jnp.bfloat16)
        sums_ref[...] = jnp.zeros(sums_ref.shape, jnp.float32)

    first = pl.multiple_of(step * SOURCES, SOURCES)
    class_block = class_ref[pl.ds(first, SOURCES), :]
    gamma_block = gamma_ref[pl.ds(first, SOURCES), :]
    class_turned = class_block.T
    gamma_turned = gamma_block.T
    down = lax.broadcasted_iota(jnp.int32, (classes, count), 0) - HALF_CLASSES
    down = down.astype(jnp.float32).astype(jnp.bfloat16)
    across = lax.broadcasted_iota(jnp.int32, (count, classes), 1) - HALF_CLASSES
    across = across.astype(jnp.float32).astype(jnp.bfloat16)
    zero = jnp.zeros((), jnp.bfloat16)
    one = jnp.ones((), jnp.bfloat16)
    error_columns = []
    for pair in range(SOURCES // 2):
        tables = []
        values = []
        for b in (2 * pair, 2 * pair + 1):
            rows = rows_ref[b]
            names = class_block[b : b + 1, :].astype(jnp.bfloat16)
            gammas = gamma_block[b : b + 1, :].astype(jnp.bfloat16)
            tables.append(jnp.where(down == names, gammas, zero))
            gamma_wide = jnp.broadcast_to(gamma_turned[:, b : b + 1], (count, angles))
            values.append(jnp.concatenate([rows, gamma_wide.astype(jnp.bfloat16)], axis=1))
            names_wide = jnp.broadcast_to(class_turned[:, b : b + 1], (count, classes))
            choice = jnp.where(names_wide.astype(jnp.bfloat16) == across, one, zero)
            model = jnp.dot(choice, model_ref[...], preferred_element_type=jnp.float32)
            resid = rows.astype(jnp.float32) - gamma_wide * model
            error_columns.append(jnp.sum(resid * resid, axis=1, keepdims=True))
        sums_ref[...] += jnp.dot(
            jnp.concatenate(tables, axis=1),
            jnp.concatenate(values, axis=0),
            preferred_element_type=jnp.float32,
        )
    error_ref[pl.ds(first, SOURCES), :] = jnp.concatenate(error_columns, axis=1).T

    @pl.when(step == pl.num_programs(0) - 1)
    def _():
        sums = sums_ref[:, 0:angles]
        weights = sums_ref[:, angles : 2 * angles]
        weights_ref[...] = weights
        grads_ref[...] = sums - weights * model_ref[...].astype(jnp.float32)
        share = angles // owned
        lane = lax.broadcasted_iota(jnp.int32, (devices, angles), 1) // share
        packed = jnp.zeros((devices, angles), jnp.float32)
        for j in range(owned):
            out_ref[pl.ds(j, devices, stride=AUX), :] = grads_ref[
                pl.ds(j, devices, stride=owned), :
            ]
            mine = weights_ref[pl.ds(j, devices, stride=owned), :]
            packed = jnp.where(lane == j, mine, packed)
        out_ref[pl.ds(owned, devices, stride=AUX), :] = packed
        out_ref[pl.ds(owned + 1, devices, stride=AUX), :] = error_ref[...]
        for j in range(owned + 2, AUX):
            out_ref[pl.ds(j, devices, stride=AUX), :] = jnp.zeros((devices, angles), jnp.float32)


def class_sums(received, owned):
    devices, rows, angles = received.shape
    count = rows - AUX
    classes = owned * devices
    return pl.pallas_call(
        classes_kernel,
        out_shape=jax.ShapeDtypeStruct((devices * AUX, angles), jnp.float32),
        grid=(devices // SOURCES,),
        in_specs=[
            pl.BlockSpec((SOURCES, count, angles), lambda i: (i, 0, 0)),
            pl.BlockSpec((devices, AUX, angles), lambda i: (0, count // AUX, 0)),
        ],
        out_specs=pl.BlockSpec((devices * AUX, angles), lambda i: (0, 0)),
        scratch_shapes=[
            pltpu.VMEM((devices * AUX, angles), jnp.float32),
            pltpu.VMEM((devices, count), jnp.float32),
            pltpu.VMEM((devices, count), jnp.float32),
            pltpu.VMEM((classes, angles), jnp.bfloat16),
            pltpu.VMEM((classes, 2 * angles), jnp.float32),
            pltpu.VMEM((classes, angles), jnp.float32),
            pltpu.VMEM((classes, angles), jnp.float32),
            pltpu.VMEM((devices, count), jnp.float32),
        ],
        compiler_params=pltpu.CompilerParams(
            dimension_semantics=("arbitrary",), vmem_limit_bytes=48 << 20
        ),
        name="class_sums",
    )(received, received)


def update_kernel(back_ref, averages_ref, velocity_ref, new_averages_ref, new_velocity_ref, error_ref):
    owned, grid_rows, angles = averages_ref.shape
    share = angles // owned
    packed = back_ref[pl.ds(owned, grid_rows, stride=AUX), :]
    for j in range(owned):
        grads = back_ref[pl.ds(j, grid_rows, stride=AUX), :]
        weights = jnp.broadcast_to(packed[:, j * share : j * share + 1], (grid_rows, angles))
        old = averages_ref[j]
        step = (grads - RIDGE * old) / (weights + RIDGE)
        moved = MOMENTUM * velocity_ref[j] + step
        new_velocity_ref[j] = moved
        new_averages_ref[j] = old + RATE * moved
    parts = back_ref[pl.ds(owned + 1, grid_rows, stride=AUX), :]
    error_ref[...] = jnp.sum(parts, axis=0, keepdims=True) / (grid_rows * angles)


def update(back, averages, velocity, count):
    owned = averages.shape[0]
    grid_rows, angles = 2 * averages.shape[2], averages.shape[3]
    flat = (owned, grid_rows, angles)
    new_averages, new_velocity, errors = pl.pallas_call(
        update_kernel,
        out_shape=(
            jax.ShapeDtypeStruct(flat, jnp.float32),
            jax.ShapeDtypeStruct(flat, jnp.float32),
            jax.ShapeDtypeStruct((1, count), jnp.float32),
        ),
        compiler_params=pltpu.CompilerParams(vmem_limit_bytes=48 << 20),
        name="update",
    )(back, averages.reshape(flat), velocity.reshape(flat))
    return (
        new_averages.reshape(averages.shape),
        new_velocity.reshape(averages.shape),
        errors.reshape(count),
    )


def on_device(stack, batch_index, best_class, best_rot, best_shift, ctf, averages, velocity):
    everyone = ("dom", "cls")
    sent = align(stack, batch_index, best_class, best_rot, best_shift, ctf, averages)
    received = lax.all_to_all(sent, everyone, split_axis=0, concat_axis=0, tiled=True)
    partial = class_sums(received, averages.shape[0])
    devices = received.shape[0]
    partial = partial.reshape(devices, AUX, received.shape[2])
    back = lax.all_to_all(partial, everyone, split_axis=0, concat_axis=0, tiled=True)
    back = back.reshape(devices * AUX, received.shape[2])
    return update(back, averages, velocity, batch_index.shape[0])


def solution(mesh):
    whole = ("dom", "cls")
    in_specs = (
        P(whole, None, None, None),
        P(whole),
        P(whole),
        P(whole),
        P(whole, None),
        P(whole, None),
        P(whole, None, None, None),
        P(whole, None, None, None),
    )
    out_specs = (P(whole, None, None, None), P(whole, None, None, None), P(whole))
    return jax.shard_map(
        on_device, mesh=mesh, in_specs=in_specs, out_specs=out_specs, check_vma=False
    )
```

time: 397 us -> 126 us (0.32)
  waiting for transfers between devices: 225 us -> 0 us
  blocking collectives: 23.1 us -> 85.9 us
  matrix products: 45.9 us -> 0 us
  Pallas kernels: 0 us -> 33.6 us
  local copies, waits for them, and re-layouts: 38.1 us -> 5.7 us
  starting transfers between devices: 25.1 us -> 0 us
  other arithmetic: 22.6 us -> 0 us
  between operations: 14.9 us -> 0.66 us
    all_to_all x3 -> x0, waiting for transfers between devices: 151 us -> none  [the longest x1 146 us: on_device(): lax.all_to_all(pack(term), 'dom', split_axis=0, concat_axis=0, tiled=True)]
    all_to_all x0 -> x2, blocking collectives: none -> 85.9 us  [the longest x1 67.2 us: on_device(): lax.all_to_all(sent, everyone, split_axis=0, concat_axis=0, tiled=True)]
    all_gather x1 -> x0, waiting for transfers between devices: 47.4 us -> none  [on_device(): lax.all_gather(averages.astype(jnp.bfloat16), ('dom', 'cls'), axis=0, til...]
    dot_general x8 -> x0, matrix products: 45.9 us -> none  [the longest x1 13.6 us: on_device(): jnp.dot(chooser, every.reshape(total_classes, flat), preferred_element_ty...]
    pallas_call x0 -> x3, Pallas kernels: none -> 33.6 us  [the longest x1 20 us: class_sums(): pl.pallas_call(classes_kernel, out_shape=jax.ShapeDtypeStruct((devices *...]
    unnamed x3 -> x0, waiting for transfers between devices: 26.9 us -> none
    all_to_all x3 -> x0, starting transfers between devices: 25 us -> none  [the longest x1 10.8 us: on_device(): lax.all_to_all(ctf_packed, 'dom', split_axis=0, concat_axis=0, tiled=True)]
    reshape x1 -> x0, local copies, waits for them, and re-layouts: 23.9 us -> none  [on_device(): every.reshape(total_classes, flat)]
  transfers between devices with their start and end apart: 5 -> 0, of which waited for: 4 -> 0; matrix products, arithmetic and copies ran while one was open for 24% -> 0% of each run, Pallas kernels for 0% -> 0%
where the time goes in v1:
time: 126 us
  blocking collectives  85.9 us (68%)
  Pallas kernels  33.6 us (27%)
  local copies, waits for them, and re-layouts  5.7 us (5%)
    all_to_all x1, blocking collectives, on_device(): lax.all_to_all(sent, everyone, split_axis=0, concat_axis=0, tiled=True)  67.2 us
    pallas_call x1, Pallas kernels, class_sums(): pl.pallas_call(classes_kernel, out_shape=jax.ShapeDtypeStruct((devices *...  20 us
    all_to_all x1, blocking collectives, on_device(): lax.all_to_all(partial, everyone, split_axis=0, concat_axis=0, tiled=True)  18.7 us
    pallas_call x1, Pallas kernels, align(): pl.pallas_call(align_kernel, out_shape=jax.ShapeDtypeStruct((grid_rows, c...  12.6 us
    unnamed x17, local copies, waits for them, and re-layouts  5.7 us

profile of v1, /device:TPU:1, one launch (start us, length us, event | category | flops | bytes accessed | tf_op | source)
XLA Modules:
  0.0 125.8 jit_solution(5564165612276776195)
XLA Ops:
  0.6 0.8 copy.12.refs_17_
  1.5 0.0 copy-start
  1.5 1.3 %copy-done = f32[2,9,2,64,128]{4,3,2,1,0:T(8,128)S(1)} copy-done((f32[2,9,2,64,128]{4,3,2,1,0:T(8,128)S(1)}, f32[2,9,2,64,128]{4,3,2,1,0:T(8,128)}, u32[]{:S(2)}) %copy-start) | copy-done | bytes 1179672
  2.7 0.0 copy-start.1
  2.7 0.9 copy-done.1
  3.7 0.0 copy-start.4
  3.7 0.7 copy-done.4
  4.4 0.0 copy-start.5
  4.4 0.7 copy-done.5
  5.0 0.0 copy-start.6
  5.0 0.7 copy-done.6
  5.7 0.0 copy-start.7
  5.7 0.7 copy-done.7
  6.3 12.6 %align.1 = bf16[128,136,128]{2,1,0:T(8,128)(2,1)S(1)} custom-call(s32[128]{0:T(128)S(1)} %copy-done.5, s32[128]{0:T(128)S(1)} %copy-done.6, s32[2,128]{1,0:T(2,128)S(1)} %bitcast.14, bf16[256,2,64,128]{3,2,1,0:T(8,128)(2,1)} %refs_15_.1, bf16[256,2,64,128]{3,2,1,0:T(8,128)(2,1)} %refs_15_.1, bf16[256,2,64,128]{3,2,1,0:T(8,128)(2,1)} %refs_15_.1, ...), custom_call_target="tpu_custom_call" | custom-call | tf_op jit(solution)/shard_map/align/pallas_call | solution.py:101
  18.9 67.2 %all_to_all.10.rows_ref.aux_ref = bf16[128,136,128]{2,1,0:T(8,128)(2,1)S(1)} all-to-all(bf16[128,136,128]{2,1,0:T(8,128)(2,1)S(1)} %align.1), channel_id=1, replica_groups=mesh['dom'=16,'cls'=8] {'dom','cls'}, dimensions={0} | all-to-all | bytes 8912896 | tf_op jit(solution)/shard_map/all_to_all | solution.py:289
  86.1 0.0 copy-start.2
  86.1 0.0 copy-start.3
  86.1 20.0 %class_sums.1 = f32[1024,128]{1,0:T(8,128)S(1)} custom-call(bf16[128,136,128]{2,1,0:T(8,128)(2,1)S(1)} %all_to_all.10.rows_ref.aux_ref, bf16[128,136,128]{2,1,0:T(8,128)(2,1)S(1)} %all_to_all.10.rows_ref.aux_ref), custom_call_target="tpu_custom_call" | custom-call | tf_op jit(solution)/shard_map/class_sums/pallas_call | solution.py:223
  106.1 18.7 %all_to_all.11 = f32[128,8,128]{2,1,0:T(8,128)S(1)} all-to-all(f32[128,8,128]{2,1,0:T(8,128)S(1)} %bitcast.9), channel_id=1, replica_groups=mesh['dom'=16,'cls'=8] {'dom','cls'}, dimensions={0} | all-to-all | bytes 1048576 | tf_op jit(solution)/shard_map/all_to_all | solution.py:293
  124.9 0.0 copy-done.2
  124.9 0.0 copy-done.3
  124.9 1.0 update.1
Async XLA Ops:
  1.5 1.3 %copy-start = (f32[2,9,2,64,128]{4,3,2,1,0:T(8,128)S(1)}, f32[2,9,2,64,128]{4,3,2,1,0:T(8,128)}, u32[]{:S(2)}) copy-start(f32[2,9,2,64,128]{4,3,2,1,0:T(8,128)} %constant.2.clone.refs_16_) | copy-start | bytes 3538948
  2.7 0.9 copy-start.1
  3.7 0.7 copy-start.4
  4.4 0.7 copy-start.5
  5.0 0.7 copy-start.6
  5.7 0.7 copy-start.7
  86.1 38.8 %copy-start.2 = (f32[4,2,64,128]{3,2,1,0:T(8,128)S(1)}, f32[4,2,64,128]{3,2,1,0:T(8,128)}, u32[]{:S(2)}) copy-start(f32[4,2,64,128]{3,2,1,0:T(8,128)} %param.15) | copy-start | bytes 786436
  86.1 38.8 %copy-start.3 = (f32[4,2,64,128]{3,2,1,0:T(8,128)S(1)}, f32[4,2,64,128]{3,2,1,0:T(8,128)}, u32[]{:S(2)}) copy-start(f32[4,2,64,128]{3,2,1,0:T(8,128)} %param.16) | copy-start | bytes 786436

commit v2 on v1

v2 whole, which is shorter than its diff:
```python
import numpy as np
import jax
import jax.numpy as jnp
from jax import lax
from jax.experimental import pallas as pl
from jax.experimental.pallas import tpu as pltpu
from jax.sharding import PartitionSpec as P

IMG = 128
TOP_SHIFT = 4
MOMENTUM = 0.9
RATE = 0.5
RIDGE = 1.0
BATCH = 16
SOURCES = 16
AUX = 8
PAD = 8
TILE = 16
HALF_CLASSES = 256


def phase_tables(cycles, angles):
    radius = np.arange(1, cycles + 1, dtype=np.float64)[:, None]
    theta = 2.0 * np.pi * np.arange(angles, dtype=np.float64)[None, :] / angles
    shifts = np.arange(-TOP_SHIFT, TOP_SHIFT + 1, dtype=np.float64)[:, None, None]
    tables = []
    for along in (np.cos(theta), np.sin(theta)):
        phase = 2.0 * np.pi * radius * along / IMG * shifts
        tables.append(np.stack([np.cos(phase), np.sin(phase)], axis=1))
    return np.stack(tables).astype(np.float32)


def align_kernel(
    index_hbm,
    rot_hbm,
    shift_hbm,
    stack_hbm,
    table_hbm,
    ctf_hbm,
    class_hbm,
    averages_hbm,
    out_ref,
    rows_ref,
    turned_ref,
    table_ref,
    index_ref,
    rot_ref,
    shift_ref,
    ctf_ref,
    class_ref,
    averages_ref,
    row_sems,
    sems,
):
    cycles, angles = table_ref.shape[3], table_ref.shape[4]
    grid_rows = 2 * cycles
    count = rows_ref.shape[0]
    chunks = count // BATCH
    owned = averages_ref.shape[0]
    pitch = grid_rows + PAD
    pairs = (
        (index_hbm, index_ref),
        (table_hbm, table_ref),
        (rot_hbm, rot_ref),
        (shift_hbm, shift_ref),
        (ctf_hbm, ctf_ref),
        (class_hbm, class_ref),
        (averages_hbm, averages_ref),
    )
    copies = [pltpu.make_async_copy(a, b, sems.at[n]) for n, (a, b) in enumerate(pairs)]
    for copy in copies:
        copy.start()
    copies[0].wait()

    def issue(i, carry):
        for j in range(BATCH):
            pltpu.make_async_copy(
                stack_hbm.at[index_ref[i * BATCH + j]], rows_ref.at[i * BATCH + j], row_sems.at[i]
            ).start()
        return carry

    lax.fori_loop(0, chunks, issue, 0)
    for copy in copies[2:]:
        copy.wait()

    classes = (class_ref[...] - HALF_CLASSES).astype(jnp.float32)
    gamma = ctf_ref[...].astype(jnp.float32)
    turned_ref[0:grid_rows, :] = jnp.broadcast_to(classes, (grid_rows, angles))
    turned_ref[pitch : pitch + cycles, :] = gamma
    turned_ref[pitch + cycles : pitch + grid_rows, :] = gamma
    for j in range(owned):
        turned_ref[(2 + j) * pitch : (2 + j) * pitch + grid_rows, :] = averages_ref[j]
    for j in range(2 + owned, AUX):
        turned_ref[j * pitch : j * pitch + grid_rows, :] = jnp.zeros(
            (grid_rows, angles), jnp.float32
        )

    def spread_aux(r, carry):
        got = turned_ref[pl.ds(r, AUX, stride=pitch), :]
        out_ref[r, pl.ds(count, AUX), :] = got.astype(jnp.bfloat16)
        return carry

    lax.fori_loop(0, grid_rows, spread_aux, 0, unroll=32)
    copies[1].wait()

    def chunk(i, carry):
        first = pl.multiple_of(i * BATCH, BATCH)
        pltpu.make_async_copy(
            stack_hbm.at[pl.ds(0, BATCH)], rows_ref.at[pl.ds(first, BATCH)], row_sems.at[i]
        ).wait()
        for j in range(BATCH):
            particle = i * BATCH + j
            sx = shift_ref[0, particle] + TOP_SHIFT
            sy = shift_ref[1, particle] + TOP_SHIFT
            back = (angles - 2 * rot_ref[particle]) % angles
            xr, xi = table_ref[0, sx, 0], table_ref[0, sx, 1]
            yr, yi = table_ref[1, sy, 0], table_ref[1, sy, 1]
            cosine = xr * yr - xi * yi
            sine = xr * yi + xi * yr
            real = rows_ref[particle, 0].astype(jnp.float32)
            imag = rows_ref[particle, 1].astype(jnp.float32)
            base = j * pitch
            turned_ref[base : base + cycles, :] = pltpu.roll(
                cosine * real - sine * imag, back, 1
            )
            turned_ref[base + cycles : base + grid_rows, :] = pltpu.roll(
                sine * real + cosine * imag, back, 1
            )

        def spread(r, inner):
            got = turned_ref[pl.ds(r, BATCH, stride=pitch), :]
            out_ref[r, pl.ds(first, BATCH), :] = got.astype(jnp.bfloat16)
            return inner

        lax.fori_loop(0, grid_rows, spread, 0, unroll=32)
        return carry

    lax.fori_loop(0, chunks, chunk, 0)


def align(stack, batch_index, best_class, best_rot, best_shift, ctf, averages):
    count = batch_index.shape[0]
    cycles, angles = stack.shape[2], stack.shape[3]
    grid_rows = 2 * cycles
    owned = averages.shape[0]
    table = jnp.asarray(phase_tables(cycles, angles))
    operands = (
        batch_index,
        best_rot,
        best_shift.T,
        stack,
        table,
        ctf.T,
        best_class.reshape(1, count),
        averages.reshape(owned, grid_rows, angles),
    )
    return pl.pallas_call(
        align_kernel,
        out_shape=jax.ShapeDtypeStruct((grid_rows, count + AUX, angles), jnp.bfloat16),
        in_specs=[pl.BlockSpec(memory_space=pltpu.HBM)] * len(operands),
        out_specs=pl.BlockSpec(memory_space=pltpu.VMEM),
        scratch_shapes=[
            pltpu.VMEM((count, 2, cycles, angles), jnp.bfloat16),
            pltpu.VMEM((BATCH * (grid_rows + PAD), angles), jnp.float32),
            pltpu.VMEM(table.shape, jnp.float32),
            pltpu.SMEM((count,), jnp.int32),
            pltpu.SMEM((count,), jnp.int32),
            pltpu.SMEM((2, count), jnp.int32),
            pltpu.VMEM((cycles, count), jnp.bfloat16),
            pltpu.VMEM((1, count), jnp.int32),
            pltpu.VMEM((owned, grid_rows, angles), jnp.float32),
            pltpu.SemaphoreType.DMA((count // BATCH,)),
            pltpu.SemaphoreType.DMA((7,)),
        ],
        compiler_params=pltpu.CompilerParams(vmem_limit_bytes=48 << 20),
        name="align",
    )(*[pltpu.with_memory_space_constraint(x, pltpu.HBM) for x in operands])


def classes_kernel(
    rows_ref,
    aux_ref,
    out_ref,
    aux32_ref,
    class_ref,
    gamma_ref,
    model_ref,
    turned_model_ref,
    sums_ref,
    grads_ref,
    weights_ref,
    error_ref,
):
    step = pl.program_id(0)
    devices, angles = aux_ref.shape[0], aux_ref.shape[2]
    count = rows_ref.shape[1]
    classes = model_ref.shape[0]
    owned = classes // devices

    @pl.when(step == 0)
    def _():
        aux32_ref[...] = aux_ref[...].astype(jnp.float32).reshape(devices * AUX, angles)
        class_ref[...] = aux32_ref[pl.ds(0, devices, stride=AUX), :]
        gamma_ref[...] = aux32_ref[pl.ds(1, devices, stride=AUX), :]
        for j in range(owned):
            model_ref[pl.ds(j, devices, stride=owned), :] = aux32_ref[
                pl.ds(2 + j, devices, stride=AUX), :
            ]
        turned_model_ref[...] = model_ref[...].T.astype(jnp.bfloat16)
        sums_ref[...] = jnp.zeros(sums_ref.shape, jnp.float32)

    first = pl.multiple_of(step * SOURCES, SOURCES)
    class_block = class_ref[pl.ds(first, SOURCES), :]
    gamma_block = gamma_ref[pl.ds(first, SOURCES), :]
    down = lax.broadcasted_iota(jnp.int32, (classes, count), 0) - HALF_CLASSES
    down = down.astype(jnp.float32).astype(jnp.bfloat16)
    zero = jnp.zeros((), jnp.bfloat16)
    last_dims = (((1,), (1,)), ((), ()))
    errors = []
    for pair in range(SOURCES // 2):
        tables = []
        gammas = []
        for b in (2 * pair, 2 * pair + 1):
            name = class_block[b : b + 1, :].astype(jnp.bfloat16)
            gamma = gamma_block[b : b + 1, :]
            tables.append(jnp.where(down == name, gamma.astype(jnp.bfloat16), zero))
            gammas.append(jnp.broadcast_to(gamma, (TILE, count)))
        table = jnp.concatenate(tables, axis=1)
        rows = rows_ref[2 * pair : 2 * pair + 2].reshape(2 * count, angles)
        turned = rows.astype(jnp.float32).T
        resid = turned - jnp.dot(
            turned_model_ref[...], table, preferred_element_type=jnp.float32
        )
        error = jnp.sum(resid * resid, axis=0, keepdims=True)
        errors += [error[:, 0:count], error[:, count : 2 * count]]
        values = jnp.concatenate([turned, jnp.concatenate(gammas, axis=1)], axis=0)
        sums_ref[...] += lax.dot_general(
            values.astype(jnp.bfloat16), table, last_dims, preferred_element_type=jnp.float32
        )
    error_ref[pl.ds(first, SOURCES), :] = jnp.concatenate(errors, axis=0)

    @pl.when(step == pl.num_programs(0) - 1)
    def _():
        weights = jnp.broadcast_to(sums_ref[angles : angles + 1, :], (angles, classes)).T
        weights_ref[...] = weights
        grads_ref[...] = sums_ref[0:angles, :].T - weights * model_ref[...]
        share = angles // owned
        lane = lax.broadcasted_iota(jnp.int32, (devices, angles), 1) // share
        packed = jnp.zeros((devices, angles), jnp.float32)
        for j in range(owned):
            out_ref[pl.ds(j, devices, stride=AUX), :] = grads_ref[
                pl.ds(j, devices, stride=owned), :
            ]
            mine = weights_ref[pl.ds(j, devices, stride=owned), :]
            packed = jnp.where(lane == j, mine, packed)
        out_ref[pl.ds(owned, devices, stride=AUX), :] = packed
        out_ref[pl.ds(owned + 1, devices, stride=AUX), :] = error_ref[...]
        for j in range(owned + 2, AUX):
            out_ref[pl.ds(j, devices, stride=AUX), :] = jnp.zeros((devices, angles), jnp.float32)


def class_sums(received, owned):
    devices, rows, angles = received.shape
    count = rows - AUX
    classes = owned * devices
    return pl.pallas_call(
        classes_kernel,
        out_shape=jax.ShapeDtypeStruct((devices * AUX, angles), jnp.float32),
        grid=(devices // SOURCES,),
        in_specs=[
            pl.BlockSpec((SOURCES, count, angles), lambda i: (i, 0, 0)),
            pl.BlockSpec((devices, AUX, angles), lambda i: (0, count // AUX, 0)),
        ],
        out_specs=pl.BlockSpec((devices * AUX, angles), lambda i: (0, 0)),
        scratch_shapes=[
            pltpu.VMEM((devices * AUX, angles), jnp.float32),
            pltpu.VMEM((devices, count), jnp.float32),
            pltpu.VMEM((devices, count), jnp.float32),
            pltpu.VMEM((classes, angles), jnp.float32),
            pltpu.VMEM((angles, classes), jnp.bfloat16),
            pltpu.VMEM((angles + TILE, classes), jnp.float32),
            pltpu.VMEM((classes, angles), jnp.float32),
            pltpu.VMEM((classes, angles), jnp.float32),
            pltpu.VMEM((devices, count), jnp.float32),
        ],
        compiler_params=pltpu.CompilerParams(
            dimension_semantics=("arbitrary",), vmem_limit_bytes=48 << 20
        ),
        name="class_sums",
    )(received, received)


def update_kernel(back_ref, averages_ref, velocity_ref, new_averages_ref, new_velocity_ref, error_ref):
    owned, grid_rows, angles = averages_ref.shape
    share = angles // owned
    packed = back_ref[pl.ds(owned, grid_rows, stride=AUX), :]
    for j in range(owned):
        grads = back_ref[pl.ds(j, grid_rows, stride=AUX), :]
        weights = jnp.broadcast_to(packed[:, j * share : j * share + 1], (grid_rows, angles))
        old = averages_ref[j]
        step = (grads - RIDGE * old) / (weights + RIDGE)
        moved = MOMENTUM * velocity_ref[j] + step
        new_velocity_ref[j] = moved
        new_averages_ref[j] = old + RATE * moved
    parts = back_ref[pl.ds(owned + 1, grid_rows, stride=AUX), :]
    error_ref[...] = jnp.sum(parts, axis=0, keepdims=True) / (grid_rows * angles)


def update(back, averages, velocity, count):
    owned = averages.shape[0]
    grid_rows, angles = 2 * averages.shape[2], averages.shape[3]
    flat = (owned, grid_rows, angles)
    new_averages, new_velocity, errors = pl.pallas_call(
        update_kernel,
        out_shape=(
            jax.ShapeDtypeStruct(flat, jnp.float32),
            jax.ShapeDtypeStruct(flat, jnp.float32),
            jax.ShapeDtypeStruct((1, count), jnp.float32),
        ),
        compiler_params=pltpu.CompilerParams(vmem_limit_bytes=48 << 20),
        name="update",
    )(back, averages.reshape(flat), velocity.reshape(flat))
    return (
        new_averages.reshape(averages.shape),
        new_velocity.reshape(averages.shape),
        errors.reshape(count),
    )


def on_device(stack, batch_index, best_class, best_rot, best_shift, ctf, averages, velocity):
    everyone = ("dom", "cls")
    sent = align(stack, batch_index, best_class, best_rot, best_shift, ctf, averages)
    received = lax.all_to_all(sent, everyone, split_axis=0, concat_axis=0, tiled=True)
    partial = class_sums(received, averages.shape[0])
    devices = received.shape[0]
    partial = partial.reshape(devices, AUX, received.shape[2])
    back = lax.all_to_all(partial, everyone, split_axis=0, concat_axis=0, tiled=True)
    back = back.reshape(devices * AUX, received.shape[2])
    return update(back, averages, velocity, batch_index.shape[0])


def solution(mesh):
    whole = ("dom", "cls")
    in_specs = (
        P(whole, None, None, None),
        P(whole),
        P(whole),
        P(whole),
        P(whole, None),
        P(whole, None),
        P(whole, None, None, None),
        P(whole, None, None, None),
    )
    out_specs = (P(whole, None, None, None), P(whole, None, None, None), P(whole))
    return jax.shard_map(
        on_device, mesh=mesh, in_specs=in_specs, out_specs=out_specs, check_vma=False
    )
```

time: 126 us -> 104 us (0.83)
  Pallas kernels: 33.6 us -> 17 us
  local copies, waits for them, and re-layouts: 5.7 us -> 0.01 us
    pallas_call x1, Pallas kernels: 20 us -> 9.79 us  [class_sums(): pl.pallas_call(classes_kernel, out_shape=jax.ShapeDtypeStruct((devices *...]
    pallas_call x1, Pallas kernels: 12.6 us -> 6.23 us  [align(): pl.pallas_call(align_kernel, out_shape=jax.ShapeDtypeStruct((grid_rows, c...]
    unnamed x17 -> x4, local copies, waits for them, and re-layouts: 5.7 us -> 0.01 us
where the time goes in v2:
time: 104 us
  blocking collectives  85.9 us (83%)
  Pallas kernels  17 us (16%)
    all_to_all x1, blocking collectives, on_device(): lax.all_to_all(sent, everyone, split_axis=0, concat_axis=0, tiled=True)  67.2 us
    all_to_all x1, blocking collectives, on_device(): lax.all_to_all(partial, everyone, split_axis=0, concat_axis=0, tiled=True)  18.7 us
    pallas_call x1, Pallas kernels, class_sums(): pl.pallas_call(classes_kernel, out_shape=jax.ShapeDtypeStruct((devices *...  9.79 us
    pallas_call x1, Pallas kernels, align(): pl.pallas_call(align_kernel, out_shape=jax.ShapeDtypeStruct((grid_rows, c...  6.23 us

profile of v2, /device:TPU:1, one launch (start us, length us, event | category | flops | bytes accessed | tf_op | source)
XLA Modules:
  0.0 103.5 jit_solution(6260381366554199096)
XLA Ops:
  0.6 6.2 %align.1 = bf16[128,136,128]{2,1,0:T(8,128)(2,1)S(1)} custom-call(s32[128]{0:T(128)} %index_hbm.1, s32[128]{0:T(128)} %rot_hbm.1, s32[2,128]{1,0:T(2,128)} %bitcast.16, bf16[256,2,64,128]{3,2,1,0:T(8,128)(2,1)} %stack_hbm.1, f32[2,9,2,64,128]{4,3,2,1,0:T(8,128)} %constant.2.clone.table_hbm, bf16[64,128]{1,0:T(8,128)(2,1)} %bitcast.15, s32[1,128]{1,0:T(1,128)} %bitcast.17, ...), custom_call_target="tpu_custom_call" | custom-call | tf_op jit(solution)/shard_map/align/pallas_call | solution.py:157
  6.9 67.2 %all_to_all.10.rows_ref.aux_ref = bf16[128,136,128]{2,1,0:T(8,128)(2,1)S(1)} all-to-all(bf16[128,136,128]{2,1,0:T(8,128)(2,1)S(1)} %align.1), channel_id=1, replica_groups=mesh['dom'=16,'cls'=8] {'dom','cls'}, dimensions={0} | all-to-all | bytes 8912896 | tf_op jit(solution)/shard_map/all_to_all | solution.py:333
  74.0 0.0 copy-start
  74.0 0.0 copy-start.1
  74.0 9.8 %class_sums.1 = f32[1024,128]{1,0:T(8,128)S(1)} custom-call(bf16[128,136,128]{2,1,0:T(8,128)(2,1)S(1)} %all_to_all.10.rows_ref.aux_ref, bf16[128,136,128]{2,1,0:T(8,128)(2,1)S(1)} %all_to_all.10.rows_ref.aux_ref), custom_call_target="tpu_custom_call" | custom-call | tf_op jit(solution)/shard_map/class_sums/pallas_call | solution.py:266
  83.8 18.7 %all_to_all.11 = f32[128,8,128]{2,1,0:T(8,128)S(1)} all-to-all(f32[128,8,128]{2,1,0:T(8,128)S(1)} %bitcast.10), channel_id=1, replica_groups=mesh['dom'=16,'cls'=8] {'dom','cls'}, dimensions={0} | all-to-all | bytes 1048576 | tf_op jit(solution)/shard_map/all_to_all | solution.py:337
  102.6 0.0 copy-done
  102.6 0.0 copy-done.1
  102.6 1.0 update.1
Async XLA Ops:
  74.0 28.5 %copy-start = (f32[4,2,64,128]{3,2,1,0:T(8,128)S(1)}, f32[4,2,64,128]{3,2,1,0:T(8,128)}, u32[]{:S(2)}) copy-start(f32[4,2,64,128]{3,2,1,0:T(8,128)} %param.15) | copy-start | bytes 786436
  74.0 28.5 %copy-start.1 = (f32[4,2,64,128]{3,2,1,0:T(8,128)S(1)}, f32[4,2,64,128]{3,2,1,0:T(8,128)}, u32[]{:S(2)}) copy-start(f32[4,2,64,128]{3,2,1,0:T(8,128)} %param.16) | copy-start | bytes 786436

commit v3 on v2

--- a/solution.py
+++ b/solution.py
@@ -42,6 +42,7 @@
     out_ref,
     rows_ref,
     turned_ref,
+    other_ref,
     table_ref,
     index_ref,
     rot_ref,
@@ -103,13 +104,13 @@
     lax.fori_loop(0, grid_rows, spread_aux, 0, unroll=32)
     copies[1].wait()
 
-    def chunk(i, carry):
-        first = pl.multiple_of(i * BATCH, BATCH)
+    def turn(i, turned):
+        first = i * BATCH
         pltpu.make_async_copy(
             stack_hbm.at[pl.ds(0, BATCH)], rows_ref.at[pl.ds(first, BATCH)], row_sems.at[i]
         ).wait()
         for j in range(BATCH):
-            particle = i * BATCH + j
+            particle = first + j
             sx = shift_ref[0, particle] + TOP_SHIFT
             sy = shift_ref[1, particle] + TOP_SHIFT
             back = (angles - 2 * rot_ref[particle]) % angles
@@ -120,22 +121,30 @@
             real = rows_ref[particle, 0].astype(jnp.float32)
             imag = rows_ref[particle, 1].astype(jnp.float32)
             base = j * pitch
-            turned_ref[base : base + cycles, :] = pltpu.roll(
-                cosine * real - sine * imag, back, 1
-            )
-            turned_ref[base + cycles : base + grid_rows, :] = pltpu.roll(
+            turned[base : base + cycles, :] = pltpu.roll(cosine * real - sine * imag, back, 1)
+            turned[base + cycles : base + grid_rows, :] = pltpu.roll(
                 sine * real + cosine * imag, back, 1
             )
 
-        def spread(r, inner):
-            got = turned_ref[pl.ds(r, BATCH, stride=pitch), :]
+    def spread(i, turned):
+        first = pl.multiple_of(i * BATCH, BATCH)
+        for r in range(grid_rows):
+            got = turned[pl.ds(r, BATCH, stride=pitch), :]
             out_ref[r, pl.ds(first, BATCH), :] = got.astype(jnp.bfloat16)
-            return inner
-
-        lax.fori_loop(0, grid_rows, spread, 0, unroll=32)
+
+    turn(0, turned_ref)
+
+    def two(h, carry):
+        turn(2 * h + 1, other_ref)
+        spread(2 * h, turned_ref)
+        turn(2 * h + 2, turned_ref)
+        spread(2 * h + 1, other_ref)
         return carry
 
-    lax.fori_loop(0, chunks, chunk, 0)
+    lax.fori_loop(0, chunks // 2 - 1, two, 0)
+    turn(chunks - 1, other_ref)
+    spread(chunks - 2, turned_ref)
+    spread(chunks - 1, other_ref)
 
 
 def align(stack, batch_index, best_class, best_rot, best_shift, ctf, averages):
@@ -162,6 +171,7 @@
         scratch_shapes=[
             pltpu.VMEM((count, 2, cycles, angles), jnp.bfloat16),
             pltpu.VMEM((BATCH * (grid_rows + PAD), angles), jnp.float32),
+            pltpu.VMEM((BATCH * (grid_rows + PAD), angles), jnp.float32),
             pltpu.VMEM(table.shape, jnp.float32),
             pltpu.SMEM((count,), jnp.int32),
             pltpu.SMEM((count,), jnp.int32),
@@ -178,8 +188,7 @@
 
 
 def classes_kernel(
-    rows_ref,
-    aux_ref,
+    received_ref,
     out_ref,
     aux32_ref,
     class_ref,
@@ -191,87 +200,78 @@
     weights_ref,
     error_ref,
 ):
-    step = pl.program_id(0)
-    devices, angles = aux_ref.shape[0], aux_ref.shape[2]
-    count = rows_ref.shape[1]
+    devices, height, angles = received_ref.shape
+    count = height - AUX
     classes = model_ref.shape[0]
     owned = classes // devices
-
-    @pl.when(step == 0)
-    def _():
-        aux32_ref[...] = aux_ref[...].astype(jnp.float32).reshape(devices * AUX, angles)
-        class_ref[...] = aux32_ref[pl.ds(0, devices, stride=AUX), :]
-        gamma_ref[...] = aux32_ref[pl.ds(1, devices, stride=AUX), :]
-        for j in range(owned):
-            model_ref[pl.ds(j, devices, stride=owned), :] = aux32_ref[
-                pl.ds(2 + j, devices, stride=AUX), :
-            ]
-        turned_model_ref[...] = model_ref[...].T.astype(jnp.bfloat16)
-        sums_ref[...] = jnp.zeros(sums_ref.shape, jnp.float32)
-
-    first = pl.multiple_of(step * SOURCES, SOURCES)
-    class_block = class_ref[pl.ds(first, SOURCES), :]
-    gamma_block = gamma_ref[pl.ds(first, SOURCES), :]
-    down = lax.broadcasted_iota(jnp.int32, (classes, count), 0) - HALF_CLASSES
-    down = down.astype(jnp.float32).astype(jnp.bfloat16)
-    zero = jnp.zeros((), jnp.bfloat16)
-    last_dims = (((1,), (1,)), ((), ()))
-    errors = []
-    for pair in range(SOURCES // 2):
-        tables = []
-        gammas = []
-        for b in (2 * pair, 2 * pair + 1):
-            name = class_block[b : b + 1, :].astype(jnp.bfloat16)
-            gamma = gamma_block[b : b + 1, :]
-            tables.append(jnp.where(down == name, gamma.astype(jnp.bfloat16), zero))
-            gammas.append(jnp.broadcast_to(gamma, (TILE, count)))
-        table = jnp.concatenate(tables, axis=1)
-        rows = rows_ref[2 * pair : 2 * pair + 2].reshape(2 * count, angles)
-        turned = rows.astype(jnp.float32).T
-        resid = turned - jnp.dot(
-            turned_model_ref[...], table, preferred_element_type=jnp.float32
-        )
-        error = jnp.sum(resid * resid, axis=0, keepdims=True)
-        errors += [error[:, 0:count], error[:, count : 2 * count]]
-        values = jnp.concatenate([turned, jnp.concatenate(gammas, axis=1)], axis=0)
-        sums_ref[...] += lax.dot_general(
-            values.astype(jnp.bfloat16), table, last_dims, preferred_element_type=jnp.float32
-        )
-    error_ref[pl.ds(first, SOURCES), :] = jnp.concatenate(errors, axis=0)
-
-    @pl.when(step == pl.num_programs(0) - 1)
-    def _():
-        weights = jnp.broadcast_to(sums_ref[angles : angles + 1, :], (angles, classes)).T
-        weights_ref[...] = weights
-        grads_ref[...] = sums_ref[0:angles, :].T - weights * model_ref[...]
-        share = angles // owned
-        lane = lax.broadcasted_iota(jnp.int32, (devices, angles), 1) // share
-        packed = jnp.zeros((devices, angles), jnp.float32)
-        for j in range(owned):
-            out_ref[pl.ds(j, devices, stride=AUX), :] = grads_ref[
-                pl.ds(j, devices, stride=owned), :
-            ]
-            mine = weights_ref[pl.ds(j, devices, stride=owned), :]
-            packed = jnp.where(lane == j, mine, packed)
-        out_ref[pl.ds(owned, devices, stride=AUX), :] = packed
-        out_ref[pl.ds(owned + 1, devices, stride=AUX), :] = error_ref[...]
-        for j in range(owned + 2, AUX):
-            out_ref[pl.ds(j, devices, stride=AUX), :] = jnp.zeros((devices, angles), jnp.float32)
+    aux = received_ref[:, count:height, :]
+    aux32_ref[...] = aux.astype(jnp.float32).reshape(devices * AUX, angles)
+    class_ref[...] = aux32_ref[pl.ds(0, devices, stride=AUX), :]
+    gamma_ref[...] = aux32_ref[pl.ds(1, devices, stride=AUX), :]
+    for j in range(owned):
+        model_ref[pl.ds(j, devices, stride=owned), :] = aux32_ref[
+            pl.ds(2 + j, devices, stride=AUX), :
+        ]
+    turned_model_ref[...] = model_ref[...].T.astype(jnp.bfloat16)
+    sums_ref[...] = jnp.zeros(sums_ref.shape, jnp.float32)
+
+    def step(i, carry):
+        first = pl.multiple_of(i * SOURCES, SOURCES)
+        class_block = class_ref[pl.ds(first, SOURCES), :]
+        gamma_block = gamma_ref[pl.ds(first, SOURCES), :]
+        down = lax.broadcasted_iota(jnp.int32, (classes, count), 0) - HALF_CLASSES
+        down = down.astype(jnp.float32).astype(jnp.bfloat16)
+        zero = jnp.zeros((), jnp.bfloat16)
+        last_dims = (((1,), (1,)), ((), ()))
+        errors = []
+        for pair in range(SOURCES // 2):
+            tables = []
+            gammas = []
+            for b in (2 * pair, 2 * pair + 1):
+                name = class_block[b : b + 1, :].astype(jnp.bfloat16)
+                gamma = gamma_block[b : b + 1, :]
+                tables.append(jnp.where(down == name, gamma.astype(jnp.bfloat16), zero))
+                gammas.append(jnp.broadcast_to(gamma, (TILE, count)))
+            table = jnp.concatenate(tables, axis=1)
+            rows = received_ref[pl.ds(first + 2 * pair, 2), 0:count, :].reshape(2 * count, angles)
+            turned = rows.astype(jnp.float32).T
+            resid = turned - jnp.dot(
+                turned_model_ref[...], table, preferred_element_type=jnp.float32
+            )
+            error = jnp.sum(resid * resid, axis=0, keepdims=True)
+            errors += [error[:, 0:count], error[:, count : 2 * count]]
+            values = jnp.concatenate([turned, jnp.concatenate(gammas, axis=1)], axis=0)
+            sums_ref[...] += lax.dot_general(
+                values.astype(jnp.bfloat16), table, last_dims, preferred_element_type=jnp.float32
+            )
+        error_ref[pl.ds(first, SOURCES), :] = jnp.concatenate(errors, axis=0)
+        return carry
+
+    lax.fori_loop(0, devices // SOURCES, step, 0)
+
+    weights = jnp.broadcast_to(sums_ref[angles : angles + 1, :], (angles, classes)).T
+    weights_ref[...] = weights
+    grads_ref[...] = sums_ref[0:angles, :].T - weights * model_ref[...]
+    share = angles // owned
+    lane = lax.broadcasted_iota(jnp.int32, (devices, angles), 1) // share
+    packed = jnp.zeros((devices, angles), jnp.float32)
+    back = owned + 2
+    for j in range(owned):
+        out_ref[pl.ds(j, devices, stride=back), :] = grads_ref[pl.ds(j, devices, stride=owned), :]
+        packed = jnp.where(lane == j, weights_ref[pl.ds(j, devices, stride=owned), :], packed)
+    out_ref[pl.ds(owned, devices, stride=back), :] = packed
+    out_ref[pl.ds(owned + 1, devices, stride=back), :] = error_ref[...]
 
 
 def class_sums(received, owned):
-    devices, rows, angles = received.shape
-    count = rows - AUX
+    devices, height, angles = received.shape
+    count = height - AUX
     classes = owned * devices
     return pl.pallas_call(
         classes_kernel,
-        out_shape=jax.ShapeDtypeStruct((devices * AUX, angles), jnp.float32),
-        grid=(devices // SOURCES,),
-        in_specs=[
-            pl.BlockSpec((SOURCES, count, angles), lambda i: (i, 0, 0)),
-            pl.BlockSpec((devices, AUX, angles), lambda i: (0, count // AUX, 0)),
-        ],
-        out_specs=pl.BlockSpec((devices * AUX, angles), lambda i: (0, 0)),
+        out_shape=jax.ShapeDtypeStruct((devices * (owned + 2), angles), jnp.float32),
+        in_specs=[pl.BlockSpec(memory_space=pltpu.VMEM)],
+        out_specs=pl.BlockSpec(memory_space=pltpu.VMEM),
         scratch_shapes=[
             pltpu.VMEM((devices * AUX, angles), jnp.float32),
             pltpu.VMEM((devices, count), jnp.float32),
@@ -283,26 +283,25 @@
             pltpu.VMEM((classes, angles), jnp.float32),
             pltpu.VMEM((devices, count), jnp.float32),
         ],
-        compiler_params=pltpu.CompilerParams(
-            dimension_semantics=("arbitrary",), vmem_limit_bytes=48 << 20
-        ),
+        compiler_params=pltpu.CompilerParams(vmem_limit_bytes=48 << 20),
         name="class_sums",
-    )(received, received)
+    )(received)
 
 
 def update_kernel(back_ref, averages_ref, velocity_ref, new_averages_ref, new_velocity_ref, error_ref):
     owned, grid_rows, angles = averages_ref.shape
     share = angles // owned
-    packed = back_ref[pl.ds(owned, grid_rows, stride=AUX), :]
+    pitch = owned + 2
+    packed = back_ref[pl.ds(owned, grid_rows, stride=pitch), :]
     for j in range(owned):
-        grads = back_ref[pl.ds(j, grid_rows, stride=AUX), :]
+        grads = back_ref[pl.ds(j, grid_rows, stride=pitch), :]
         weights = jnp.broadcast_to(packed[:, j * share : j * share + 1], (grid_rows, angles))
         old = averages_ref[j]
         step = (grads - RIDGE * old) / (weights + RIDGE)
         moved = MOMENTUM * velocity_ref[j] + step
         new_velocity_ref[j] = moved
         new_averages_ref[j] = old + RATE * moved
-    parts = back_ref[pl.ds(owned + 1, grid_rows, stride=AUX), :]
+    parts = back_ref[pl.ds(owned + 1, grid_rows, stride=pitch), :]
     error_ref[...] = jnp.sum(parts, axis=0, keepdims=True) / (grid_rows * angles)
 
 
@@ -332,10 +331,10 @@
     sent = align(stack, batch_index, best_class, best_rot, best_shift, ctf, averages)
     received = lax.all_to_all(sent, everyone, split_axis=0, concat_axis=0, tiled=True)
     partial = class_sums(received, averages.shape[0])
-    devices = received.shape[0]
-    partial = partial.reshape(devices, AUX, received.shape[2])
+    height, angles = partial.shape
+    partial = partial.reshape(height // 2, 2, angles)
     back = lax.all_to_all(partial, everyone, split_axis=0, concat_axis=0, tiled=True)
-    back = back.reshape(devices * AUX, received.shape[2])
+    back = back.reshape(height, angles)
     return update(back, averages, velocity, batch_index.shape[0])
 
 

time: 104 us -> 101 us (0.971)
  blocking collectives: 85.9 us -> 84.5 us
    all_to_all x1, blocking collectives: 18.7 us -> 17.3 us  [on_device(): lax.all_to_all(partial, everyone, split_axis=0, concat_axis=0, tiled=True)]
where the time goes in v3:
time: 101 us
  blocking collectives  84.5 us (84%)
  Pallas kernels  16.1 us (16%)
    all_to_all x1, blocking collectives, on_device(): lax.all_to_all(sent, everyone, split_axis=0, concat_axis=0, tiled=True)  67.2 us
    all_to_all x1, blocking collectives, on_device(): lax.all_to_all(partial, everyone, split_axis=0, concat_axis=0, tiled=True)  17.3 us
    pallas_call x1, Pallas kernels, class_sums(): pl.pallas_call(classes_kernel, out_shape=jax.ShapeDtypeStruct((devices *...  9.25 us
    pallas_call x1, Pallas kernels, align(): pl.pallas_call(align_kernel, out_shape=jax.ShapeDtypeStruct((grid_rows, c...  5.93 us

profile of v3, /device:TPU:1, one launch (start us, length us, event | category | flops | bytes accessed | tf_op | source)
XLA Modules:
  0.0 101.3 jit_solution(1410220154331882460)
XLA Ops:
  0.6 5.9 %align.1 = bf16[128,136,128]{2,1,0:T(8,128)(2,1)S(1)} custom-call(s32[128]{0:T(128)} %index_hbm.1, s32[128]{0:T(128)} %rot_hbm.1, s32[2,128]{1,0:T(2,128)} %bitcast.16, bf16[256,2,64,128]{3,2,1,0:T(8,128)(2,1)} %stack_hbm.1, f32[2,9,2,64,128]{4,3,2,1,0:T(8,128)} %constant.2.clone.table_hbm, bf16[64,128]{1,0:T(8,128)(2,1)} %bitcast.15, s32[1,128]{1,0:T(1,128)} %bitcast.17, ...), custom_call_target="tpu_custom_call" | custom-call | tf_op jit(solution)/shard_map/align/pallas_call | solution.py:166
  6.6 67.2 %all_to_all.10.received_ref = bf16[128,136,128]{2,1,0:T(8,128)(2,1)S(1)} all-to-all(bf16[128,136,128]{2,1,0:T(8,128)(2,1)S(1)} %align.1), channel_id=1, replica_groups=mesh['dom'=16,'cls'=8] {'dom','cls'}, dimensions={0} | all-to-all | bytes 8912896 | tf_op jit(solution)/shard_map/all_to_all | solution.py:332
  73.7 0.0 copy-start
  73.7 0.0 copy-start.1
  73.7 9.2 %class_sums.1 = f32[768,128]{1,0:T(8,128)S(1)} custom-call(bf16[128,136,128]{2,1,0:T(8,128)(2,1)S(1)} %all_to_all.10.received_ref), custom_call_target="tpu_custom_call" | custom-call | tf_op jit(solution)/shard_map/class_sums/pallas_call | solution.py:270
  83.0 17.3 %all_to_all.11 = f32[384,2,128]{2,1,0:T(2,128)S(1)} all-to-all(f32[384,2,128]{2,1,0:T(2,128)S(1)} %bitcast.11), channel_id=1, replica_groups=mesh['dom'=16,'cls'=8] {'dom','cls'}, dimensions={0} | all-to-all | bytes 786432 | tf_op jit(solution)/shard_map/all_to_all | solution.py:336
  100.3 0.0 copy-done
  100.3 0.0 copy-done.1
  100.3 0.9 update.1
Async XLA Ops:
  73.7 26.6 %copy-start = (f32[4,2,64,128]{3,2,1,0:T(8,128)S(1)}, f32[4,2,64,128]{3,2,1,0:T(8,128)}, u32[]{:S(2)}) copy-start(f32[4,2,64,128]{3,2,1,0:T(8,128)} %param.15) | copy-start | bytes 786436
  73.7 26.6 %copy-start.1 = (f32[4,2,64,128]{3,2,1,0:T(8,128)S(1)}, f32[4,2,64,128]{3,2,1,0:T(8,128)}, u32[]{:S(2)}) copy-start(f32[4,2,64,128]{3,2,1,0:T(8,128)} %param.16) | copy-start | bytes 786436

commit v4 on v3

--- a/solution.py
+++ b/solution.py
@@ -15,7 +15,7 @@
 SOURCES = 16
 AUX = 8
 PAD = 8
-TILE = 16
+SPARE = 8
 HALF_CLASSES = 256
 
 
@@ -73,14 +73,14 @@
         copy.start()
     copies[0].wait()
 
-    def issue(i, carry):
+    def issue(i):
         for j in range(BATCH):
             pltpu.make_async_copy(
                 stack_hbm.at[index_ref[i * BATCH + j]], rows_ref.at[i * BATCH + j], row_sems.at[i]
             ).start()
-        return carry
-
-    lax.fori_loop(0, chunks, issue, 0)
+
+    issue(0)
+    issue(1)
     for copy in copies[2:]:
         copy.wait()
 
@@ -106,6 +106,8 @@
 
     def turn(i, turned):
         first = i * BATCH
+        if i + 2 < chunks:
+            issue(i + 2)
         pltpu.make_async_copy(
             stack_hbm.at[pl.ds(0, BATCH)], rows_ref.at[pl.ds(first, BATCH)], row_sems.at[i]
         ).wait()
@@ -127,24 +129,17 @@
             )
 
     def spread(i, turned):
-        first = pl.multiple_of(i * BATCH, BATCH)
+        first = i * BATCH
         for r in range(grid_rows):
             got = turned[pl.ds(r, BATCH, stride=pitch), :]
             out_ref[r, pl.ds(first, BATCH), :] = got.astype(jnp.bfloat16)
 
-    turn(0, turned_ref)
-
-    def two(h, carry):
-        turn(2 * h + 1, other_ref)
-        spread(2 * h, turned_ref)
-        turn(2 * h + 2, turned_ref)
-        spread(2 * h + 1, other_ref)
-        return carry
-
-    lax.fori_loop(0, chunks // 2 - 1, two, 0)
-    turn(chunks - 1, other_ref)
-    spread(chunks - 2, turned_ref)
-    spread(chunks - 1, other_ref)
+    scratches = (turned_ref, other_ref)
+    turn(0, scratches[0])
+    for i in range(1, chunks):
+        turn(i, scratches[i % 2])
+        spread(i - 1, scratches[(i - 1) % 2])
+    spread(chunks - 1, scratches[(chunks - 1) % 2])
 
 
 def align(stack, batch_index, best_class, best_rot, best_shift, ctf, averages):
@@ -199,6 +194,7 @@
     grads_ref,
     weights_ref,
     error_ref,
+    table_ref,
 ):
     devices, height, angles = received_ref.shape
     count = height - AUX
@@ -222,16 +218,13 @@
         down = lax.broadcasted_iota(jnp.int32, (classes, count), 0) - HALF_CLASSES
         down = down.astype(jnp.float32).astype(jnp.bfloat16)
         zero = jnp.zeros((), jnp.bfloat16)
-        last_dims = (((1,), (1,)), ((), ()))
         errors = []
         for pair in range(SOURCES // 2):
             tables = []
-            gammas = []
             for b in (2 * pair, 2 * pair + 1):
                 name = class_block[b : b + 1, :].astype(jnp.bfloat16)
                 gamma = gamma_block[b : b + 1, :]
                 tables.append(jnp.where(down == name, gamma.astype(jnp.bfloat16), zero))
-                gammas.append(jnp.broadcast_to(gamma, (TILE, count)))
             table = jnp.concatenate(tables, axis=1)
             rows = received_ref[pl.ds(first + 2 * pair, 2), 0:count, :].reshape(2 * count, angles)
             turned = rows.astype(jnp.float32).T
@@ -240,18 +233,25 @@
             )
             error = jnp.sum(resid * resid, axis=0, keepdims=True)
             errors += [error[:, 0:count], error[:, count : 2 * count]]
-            values = jnp.concatenate([turned, jnp.concatenate(gammas, axis=1)], axis=0)
-            sums_ref[...] += lax.dot_general(
-                values.astype(jnp.bfloat16), table, last_dims, preferred_element_type=jnp.float32
-            )
+            table_ref[:, 2 * pair * count : 2 * (pair + 1) * count] = table
+        columns = [
+            jnp.broadcast_to(gamma_block[b : b + 1, :], (SPARE, count)).T for b in range(SOURCES)
+        ]
+        rows = received_ref[pl.ds(first, SOURCES), 0:count, :].reshape(SOURCES * count, angles)
+        columns = jnp.concatenate(columns, axis=0).astype(jnp.bfloat16)
+        sums_ref[...] += jnp.dot(
+            table_ref[...],
+            jnp.concatenate([rows, columns], axis=1),
+            preferred_element_type=jnp.float32,
+        )
         error_ref[pl.ds(first, SOURCES), :] = jnp.concatenate(errors, axis=0)
         return carry
 
-    lax.fori_loop(0, devices // SOURCES, step, 0)
-
-    weights = jnp.broadcast_to(sums_ref[angles : angles + 1, :], (angles, classes)).T
+    lax.fori_loop(0, devices // SOURCES, step, 0, unroll=8)
+
+    weights = jnp.broadcast_to(sums_ref[:, angles : angles + 1], (classes, angles))
     weights_ref[...] = weights
-    grads_ref[...] = sums_ref[0:angles, :].T - weights * model_ref[...]
+    grads_ref[...] = sums_ref[:, 0:angles] - weights * model_ref[...]
     share = angles // owned
     lane = lax.broadcasted_iota(jnp.int32, (devices, angles), 1) // share
     packed = jnp.zeros((devices, angles), jnp.float32)
@@ -278,10 +278,11 @@
             pltpu.VMEM((devices, count), jnp.float32),
             pltpu.VMEM((classes, angles), jnp.float32),
             pltpu.VMEM((angles, classes), jnp.bfloat16),
-            pltpu.VMEM((angles + TILE, classes), jnp.float32),
+            pltpu.VMEM((classes, angles + SPARE), jnp.float32),
             pltpu.VMEM((classes, angles), jnp.float32),
             pltpu.VMEM((classes, angles), jnp.float32),
             pltpu.VMEM((devices, count), jnp.float32),
+            pltpu.VMEM((classes, SOURCES * count), jnp.bfloat16),
         ],
         compiler_params=pltpu.CompilerParams(vmem_limit_bytes=48 << 20),
         name="class_sums",

time: 101 us -> 100 us (0.990)
  Pallas kernels: 16.1 us -> 14.6 us
    pallas_call x1, Pallas kernels: 9.25 us -> 7.78 us  [class_sums(): pl.pallas_call(classes_kernel, out_shape=jax.ShapeDtypeStruct((devices *...]
where the time goes in v4:
time: 100 us; the launch traced here: 99.8 us
  blocking collectives  84.5 us (84%)
  Pallas kernels  14.6 us (15%)
    all_to_all x1, blocking collectives, on_device(): lax.all_to_all(sent, everyone, split_axis=0, concat_axis=0, tiled=True)  67.2 us
    all_to_all x1, blocking collectives, on_device(): lax.all_to_all(partial, everyone, split_axis=0, concat_axis=0, tiled=True)  17.3 us
    pallas_call x1, Pallas kernels, class_sums(): pl.pallas_call(classes_kernel, out_shape=jax.ShapeDtypeStruct((devices *...  7.78 us
    pallas_call x1, Pallas kernels, align(): pl.pallas_call(align_kernel, out_shape=jax.ShapeDtypeStruct((grid_rows, c...  5.92 us

profile of v4, /device:TPU:1, one launch (start us, length us, event | category | flops | bytes accessed | tf_op | source)
XLA Modules:
  0.0 99.8 jit_solution(5864293611104150225)
XLA Ops:
  0.6 5.9 %align.1 = bf16[128,136,128]{2,1,0:T(8,128)(2,1)S(1)} custom-call(s32[128]{0:T(128)} %index_hbm.1, s32[128]{0:T(128)} %rot_hbm.1, s32[2,128]{1,0:T(2,128)} %bitcast.16, bf16[256,2,64,128]{3,2,1,0:T(8,128)(2,1)} %stack_hbm.1, f32[2,9,2,64,128]{4,3,2,1,0:T(8,128)} %constant.2.clone.table_hbm, bf16[64,128]{1,0:T(8,128)(2,1)} %bitcast.15, s32[1,128]{1,0:T(1,128)} %bitcast.17, ...), custom_call_target="tpu_custom_call" | custom-call | tf_op jit(solution)/shard_map/align/pallas_call | solution.py:161
  6.6 67.2 %all_to_all.10.received_ref = bf16[128,136,128]{2,1,0:T(8,128)(2,1)S(1)} all-to-all(bf16[128,136,128]{2,1,0:T(8,128)(2,1)S(1)} %align.1), channel_id=1, replica_groups=mesh['dom'=16,'cls'=8] {'dom','cls'}, dimensions={0} | all-to-all | bytes 8912896 | tf_op jit(solution)/shard_map/all_to_all | solution.py:333
  73.7 0.0 copy-start
  73.7 0.0 copy-start.1
  73.7 7.8 %class_sums.1 = f32[768,128]{1,0:T(8,128)S(1)} custom-call(bf16[128,136,128]{2,1,0:T(8,128)(2,1)S(1)} %all_to_all.10.received_ref), custom_call_target="tpu_custom_call" | custom-call | tf_op jit(solution)/shard_map/class_sums/pallas_call | solution.py:270
  81.5 17.3 %all_to_all.11 = f32[384,2,128]{2,1,0:T(2,128)S(1)} all-to-all(f32[384,2,128]{2,1,0:T(2,128)S(1)} %bitcast.11), channel_id=1, replica_groups=mesh['dom'=16,'cls'=8] {'dom','cls'}, dimensions={0} | all-to-all | bytes 786432 | tf_op jit(solution)/shard_map/all_to_all | solution.py:337
  98.8 0.0 copy-done
  98.8 0.0 copy-done.1
  98.8 0.9 update.1
Async XLA Ops:
  73.7 25.1 %copy-start = (f32[4,2,64,128]{3,2,1,0:T(8,128)S(1)}, f32[4,2,64,128]{3,2,1,0:T(8,128)}, u32[]{:S(2)}) copy-start(f32[4,2,64,128]{3,2,1,0:T(8,128)} %param.15) | copy-start | bytes 786436
  73.7 25.1 %copy-start.1 = (f32[4,2,64,128]{3,2,1,0:T(8,128)S(1)}, f32[4,2,64,128]{3,2,1,0:T(8,128)}, u32[]{:S(2)}) copy-start(f32[4,2,64,128]{3,2,1,0:T(8,128)} %param.16) | copy-start | bytes 786436

commit v5 on v4

--- a/solution.py
+++ b/solution.py
@@ -195,6 +195,7 @@
     weights_ref,
     error_ref,
     table_ref,
+    back_ref,
 ):
     devices, height, angles = received_ref.shape
     count = height - AUX
@@ -250,17 +251,26 @@
     lax.fori_loop(0, devices // SOURCES, step, 0, unroll=8)
 
     weights = jnp.broadcast_to(sums_ref[:, angles : angles + 1], (classes, angles))
-    weights_ref[...] = weights
-    grads_ref[...] = sums_ref[:, 0:angles] - weights * model_ref[...]
+    sums = sums_ref[:, 0:angles]
+    grads = sums - weights * model_ref[...]
+    raw = jnp.sum(sums * sums, axis=1, keepdims=True) < jnp.sum(
+        grads * grads, axis=1, keepdims=True
+    )
+    raw = jnp.broadcast_to(raw.astype(jnp.float32), (classes, angles))
+    grads_ref[...] = jnp.where(raw > 0.5, sums, grads)
     share = angles // owned
+    part = lax.broadcasted_iota(jnp.int32, (classes, angles), 1) % share // (share // 4)
+    high = weights.astype(jnp.bfloat16).astype(jnp.float32)
+    weights_ref[...] = jnp.where(part == 0, high, jnp.where(part == 1, weights - high, raw))
     lane = lax.broadcasted_iota(jnp.int32, (devices, angles), 1) // share
     packed = jnp.zeros((devices, angles), jnp.float32)
     back = owned + 2
     for j in range(owned):
-        out_ref[pl.ds(j, devices, stride=back), :] = grads_ref[pl.ds(j, devices, stride=owned), :]
+        back_ref[pl.ds(j, devices, stride=back), :] = grads_ref[pl.ds(j, devices, stride=owned), :]
         packed = jnp.where(lane == j, weights_ref[pl.ds(j, devices, stride=owned), :], packed)
-    out_ref[pl.ds(owned, devices, stride=back), :] = packed
-    out_ref[pl.ds(owned + 1, devices, stride=back), :] = error_ref[...]
+    back_ref[pl.ds(owned, devices, stride=back), :] = packed
+    back_ref[pl.ds(owned + 1, devices, stride=back), :] = error_ref[...]
+    out_ref[...] = back_ref[...].astype(jnp.bfloat16)
 
 
 def class_sums(received, owned):
@@ -269,7 +279,7 @@
     classes = owned * devices
     return pl.pallas_call(
         classes_kernel,
-        out_shape=jax.ShapeDtypeStruct((devices * (owned + 2), angles), jnp.float32),
+        out_shape=jax.ShapeDtypeStruct((devices * (owned + 2), angles), jnp.bfloat16),
         in_specs=[pl.BlockSpec(memory_space=pltpu.VMEM)],
         out_specs=pl.BlockSpec(memory_space=pltpu.VMEM),
         scratch_shapes=[
@@ -283,21 +293,37 @@
             pltpu.VMEM((classes, angles), jnp.float32),
             pltpu.VMEM((devices, count), jnp.float32),
             pltpu.VMEM((classes, SOURCES * count), jnp.bfloat16),
+            pltpu.VMEM((devices * (owned + 2), angles), jnp.float32),
         ],
         compiler_params=pltpu.CompilerParams(vmem_limit_bytes=48 << 20),
         name="class_sums",
     )(received)
 
 
-def update_kernel(back_ref, averages_ref, velocity_ref, new_averages_ref, new_velocity_ref, error_ref):
+def update_kernel(
+    sent_ref,
+    averages_ref,
+    velocity_ref,
+    new_averages_ref,
+    new_velocity_ref,
+    error_ref,
+    back_ref,
+):
     owned, grid_rows, angles = averages_ref.shape
     share = angles // owned
     pitch = owned + 2
+    back_ref[...] = sent_ref[...].astype(jnp.float32)
     packed = back_ref[pl.ds(owned, grid_rows, stride=pitch), :]
     for j in range(owned):
-        grads = back_ref[pl.ds(j, grid_rows, stride=pitch), :]
-        weights = jnp.broadcast_to(packed[:, j * share : j * share + 1], (grid_rows, angles))
+        base = j * share
+        high = packed[:, base : base + 1]
+        low = packed[:, base + share // 4 : base + share // 4 + 1]
+        raw = packed[:, base + share // 2 : base + share // 2 + 1]
+        weights = jnp.broadcast_to(high + low, (grid_rows, angles))
         old = averages_ref[j]
+        model = old.astype(jnp.bfloat16).astype(jnp.float32)
+        sent = back_ref[pl.ds(j, grid_rows, stride=pitch), :]
+        grads = sent - jnp.broadcast_to(raw * (high + low), (grid_rows, angles)) * model
         step = (grads - RIDGE * old) / (weights + RIDGE)
         moved = MOMENTUM * velocity_ref[j] + step
         new_velocity_ref[j] = moved
@@ -317,6 +343,7 @@
             jax.ShapeDtypeStruct(flat, jnp.float32),
             jax.ShapeDtypeStruct((1, count), jnp.float32),
         ),
+        scratch_shapes=[pltpu.VMEM(back.shape, jnp.float32)],
         compiler_params=pltpu.CompilerParams(vmem_limit_bytes=48 << 20),
         name="update",
     )(back, averages.reshape(flat), velocity.reshape(flat))

time: 100 us -> 99.4 us (level)
  blocking collectives: 84.5 us -> 82.7 us
  Pallas kernels: 14.6 us -> 15.8 us
    all_to_all x1, blocking collectives: 17.3 us -> 15.5 us  [on_device(): lax.all_to_all(partial, everyone, split_axis=0, concat_axis=0, tiled=True)]
where the time goes in v5:
time: 99.4 us; the launch traced here: 99.1 us
  blocking collectives  82.7 us (83%)
  Pallas kernels  15.8 us (16%)
    all_to_all x1, blocking collectives, on_device(): lax.all_to_all(sent, everyone, split_axis=0, concat_axis=0, tiled=True)  67.2 us
    all_to_all x1, blocking collectives, on_device(): lax.all_to_all(partial, everyone, split_axis=0, concat_axis=0, tiled=True)  15.5 us
    pallas_call x1, Pallas kernels, class_sums(): pl.pallas_call(classes_kernel, out_shape=jax.ShapeDtypeStruct((devices *...  8.72 us
    pallas_call x1, Pallas kernels, align(): pl.pallas_call(align_kernel, out_shape=jax.ShapeDtypeStruct((grid_rows, c...  5.92 us

profile of v5, /device:TPU:1, one launch (start us, length us, event | category | flops | bytes accessed | tf_op | source)
XLA Modules:
  0.0 99.1 jit_solution(7038512117586648343)
XLA Ops:
  0.6 5.9 %align.1 = bf16[128,136,128]{2,1,0:T(8,128)(2,1)S(1)} custom-call(s32[128]{0:T(128)} %index_hbm.1, s32[128]{0:T(128)} %rot_hbm.1, s32[2,128]{1,0:T(2,128)} %bitcast.16, bf16[256,2,64,128]{3,2,1,0:T(8,128)(2,1)} %stack_hbm.1, f32[2,9,2,64,128]{4,3,2,1,0:T(8,128)} %constant.2.clone.table_hbm, bf16[64,128]{1,0:T(8,128)(2,1)} %bitcast.15, s32[1,128]{1,0:T(1,128)} %bitcast.17, ...), custom_call_target="tpu_custom_call" | custom-call | tf_op jit(solution)/shard_map/align/pallas_call | solution.py:161
  6.6 67.2 %all_to_all.10.received_ref = bf16[128,136,128]{2,1,0:T(8,128)(2,1)S(1)} all-to-all(bf16[128,136,128]{2,1,0:T(8,128)(2,1)S(1)} %align.1), channel_id=1, replica_groups=mesh['dom'=16,'cls'=8] {'dom','cls'}, dimensions={0} | all-to-all | bytes 8912896 | tf_op jit(solution)/shard_map/all_to_all | solution.py:360
  73.7 0.0 copy-start
  73.7 0.0 copy-start.1
  73.7 8.7 %class_sums.1 = bf16[768,128]{1,0:T(8,128)(2,1)S(1)} custom-call(bf16[128,136,128]{2,1,0:T(8,128)(2,1)S(1)} %all_to_all.10.received_ref), custom_call_target="tpu_custom_call" | custom-call | tf_op jit(solution)/shard_map/class_sums/pallas_call | solution.py:280
  82.5 15.5 %all_to_all.11 = bf16[384,2,128]{2,1,0:T(2,128)(2,1)S(1)} all-to-all(bf16[384,2,128]{2,1,0:T(2,128)(2,1)S(1)} %bitcast.12), channel_id=1, replica_groups=mesh['dom'=16,'cls'=8] {'dom','cls'}, dimensions={0} | all-to-all | bytes 393216 | tf_op jit(solution)/shard_map/all_to_all | solution.py:364
  98.0 0.0 copy-done
  98.0 0.0 copy-done.1
  98.0 1.1 %update.1 = (f32[4,128,128]{2,1,0:T(8,128)}, f32[4,128,128]{2,1,0:T(8,128)}, f32[1,128]{1,0:T(1,128)}) custom-call(bf16[768,128]{1,0:T(8,128)(2,1)S(1)} %bitcast.13, f32[4,128,128]{2,1,0:T(8,128)S(1)} %bitcast.11, f32[4,128,128]{2,1,0:T(8,128)S(1)} %bitcast.14), custom_call_target="tpu_custom_call" | custom-call | tf_op jit(solution)/shard_map/update/pallas_call | solution.py:339
Async XLA Ops:
  73.7 24.3 %copy-start = (f32[4,2,64,128]{3,2,1,0:T(8,128)S(1)}, f32[4,2,64,128]{3,2,1,0:T(8,128)}, u32[]{:S(2)}) copy-start(f32[4,2,64,128]{3,2,1,0:T(8,128)} %param.15) | copy-start | bytes 786436
  73.7 24.3 %copy-start.1 = (f32[4,2,64,128]{3,2,1,0:T(8,128)S(1)}, f32[4,2,64,128]{3,2,1,0:T(8,128)}, u32[]{:S(2)}) copy-start(f32[4,2,64,128]{3,2,1,0:T(8,128)} %param.16) | copy-start | bytes 786436

commit v6 on v5

--- a/solution.py
+++ b/solution.py
@@ -228,7 +228,7 @@
                 tables.append(jnp.where(down == name, gamma.astype(jnp.bfloat16), zero))
             table = jnp.concatenate(tables, axis=1)
             rows = received_ref[pl.ds(first + 2 * pair, 2), 0:count, :].reshape(2 * count, angles)
-            turned = rows.astype(jnp.float32).T
+            turned = rows.T.astype(jnp.float32)
             resid = turned - jnp.dot(
                 turned_model_ref[...], table, preferred_element_type=jnp.float32
             )
@@ -252,12 +252,13 @@
 
     weights = jnp.broadcast_to(sums_ref[:, angles : angles + 1], (classes, angles))
     sums = sums_ref[:, 0:angles]
-    grads = sums - weights * model_ref[...]
-    raw = jnp.sum(sums * sums, axis=1, keepdims=True) < jnp.sum(
-        grads * grads, axis=1, keepdims=True
-    )
-    raw = jnp.broadcast_to(raw.astype(jnp.float32), (classes, angles))
-    grads_ref[...] = jnp.where(raw > 0.5, sums, grads)
+    pull = weights * model_ref[...]
+    excess = (pull * (sums + sums - pull)).astype(jnp.bfloat16)
+    excess = jnp.dot(
+        excess, jnp.ones((angles, angles), jnp.bfloat16), preferred_element_type=jnp.float32
+    )
+    raw = (excess < 0.0).astype(jnp.float32)
+    grads_ref[...] = jnp.where(excess < 0.0, sums, sums - pull)
     share = angles // owned
     part = lax.broadcasted_iota(jnp.int32, (classes, angles), 1) % share // (share // 4)
     high = weights.astype(jnp.bfloat16).astype(jnp.float32)

time: 99.4 us -> 98 us (0.986)
  Pallas kernels: 15.8 us -> 14.5 us
    pallas_call x1, Pallas kernels: 8.72 us -> 7.45 us  [class_sums(): pl.pallas_call(classes_kernel, out_shape=jax.ShapeDtypeStruct((devices *...]
where the time goes in v6:
time: 98 us; the launch traced here: 97.8 us
  blocking collectives  82.6 us (84%)
  Pallas kernels  14.5 us (15%)
    all_to_all x1, blocking collectives, on_device(): lax.all_to_all(sent, everyone, split_axis=0, concat_axis=0, tiled=True)  67.2 us
    all_to_all x1, blocking collectives, on_device(): lax.all_to_all(partial, everyone, split_axis=0, concat_axis=0, tiled=True)  15.4 us
    pallas_call x1, Pallas kernels, class_sums(): pl.pallas_call(classes_kernel, out_shape=jax.ShapeDtypeStruct((devices *...  7.45 us
    pallas_call x1, Pallas kernels, align(): pl.pallas_call(align_kernel, out_shape=jax.ShapeDtypeStruct((grid_rows, c...  5.92 us

profile of v6, /device:TPU:1, one launch (start us, length us, event | category | flops | bytes accessed | tf_op | source)
XLA Modules:
  0.0 97.8 jit_solution(14084076576634155501)
XLA Ops:
  0.6 5.9 %align.1 = bf16[128,136,128]{2,1,0:T(8,128)(2,1)S(1)} custom-call(s32[128]{0:T(128)} %index_hbm.1, s32[128]{0:T(128)} %rot_hbm.1, s32[2,128]{1,0:T(2,128)} %bitcast.16, bf16[256,2,64,128]{3,2,1,0:T(8,128)(2,1)} %stack_hbm.1, f32[2,9,2,64,128]{4,3,2,1,0:T(8,128)} %constant.2.clone.table_hbm, bf16[64,128]{1,0:T(8,128)(2,1)} %bitcast.15, s32[1,128]{1,0:T(1,128)} %bitcast.17, ...), custom_call_target="tpu_custom_call" | custom-call | tf_op jit(solution)/shard_map/align/pallas_call | solution.py:161
  6.6 67.2 %all_to_all.10.received_ref = bf16[128,136,128]{2,1,0:T(8,128)(2,1)S(1)} all-to-all(bf16[128,136,128]{2,1,0:T(8,128)(2,1)S(1)} %align.1), channel_id=1, replica_groups=mesh['dom'=16,'cls'=8] {'dom','cls'}, dimensions={0} | all-to-all | bytes 8912896 | tf_op jit(solution)/shard_map/all_to_all | solution.py:361
  73.7 0.0 copy-start
  73.7 0.0 copy-start.1
  73.7 7.5 %class_sums.1 = bf16[768,128]{1,0:T(8,128)(2,1)S(1)} custom-call(bf16[128,136,128]{2,1,0:T(8,128)(2,1)S(1)} %all_to_all.10.received_ref), custom_call_target="tpu_custom_call" | custom-call | tf_op jit(solution)/shard_map/class_sums/pallas_call | solution.py:281
  81.2 15.4 %all_to_all.11 = bf16[384,2,128]{2,1,0:T(2,128)(2,1)S(1)} all-to-all(bf16[384,2,128]{2,1,0:T(2,128)(2,1)S(1)} %bitcast.12), channel_id=1, replica_groups=mesh['dom'=16,'cls'=8] {'dom','cls'}, dimensions={0} | all-to-all | bytes 393216 | tf_op jit(solution)/shard_map/all_to_all | solution.py:365
  96.6 0.0 copy-done
  96.6 0.0 copy-done.1
  96.6 1.1 %update.1 = (f32[4,128,128]{2,1,0:T(8,128)}, f32[4,128,128]{2,1,0:T(8,128)}, f32[1,128]{1,0:T(1,128)}) custom-call(bf16[768,128]{1,0:T(8,128)(2,1)S(1)} %bitcast.13, f32[4,128,128]{2,1,0:T(8,128)S(1)} %bitcast.11, f32[4,128,128]{2,1,0:T(8,128)S(1)} %bitcast.14), custom_call_target="tpu_custom_call" | custom-call | tf_op jit(solution)/shard_map/update/pallas_call | solution.py:340
Async XLA Ops:
  73.7 22.9 %copy-start = (f32[4,2,64,128]{3,2,1,0:T(8,128)S(1)}, f32[4,2,64,128]{3,2,1,0:T(8,128)}, u32[]{:S(2)}) copy-start(f32[4,2,64,128]{3,2,1,0:T(8,128)} %param.15) | copy-start | bytes 786436
  73.7 22.9 %copy-start.1 = (f32[4,2,64,128]{3,2,1,0:T(8,128)S(1)}, f32[4,2,64,128]{3,2,1,0:T(8,128)}, u32[]{:S(2)}) copy-start(f32[4,2,64,128]{3,2,1,0:T(8,128)} %param.16) | copy-start | bytes 786436

commit v7 on v6

--- a/solution.py
+++ b/solution.py
@@ -58,7 +58,7 @@
     count = rows_ref.shape[0]
     chunks = count // BATCH
     owned = averages_ref.shape[0]
-    pitch = grid_rows + PAD
+    pitch = BATCH + PAD
     pairs = (
         (index_hbm, index_ref),
         (table_hbm, table_ref),
@@ -86,22 +86,20 @@
 
     classes = (class_ref[...] - HALF_CLASSES).astype(jnp.float32)
     gamma = ctf_ref[...].astype(jnp.float32)
-    turned_ref[0:grid_rows, :] = jnp.broadcast_to(classes, (grid_rows, angles))
-    turned_ref[pitch : pitch + cycles, :] = gamma
-    turned_ref[pitch + cycles : pitch + grid_rows, :] = gamma
+    def place(turned, row, column, values):
+        turned[pl.ds(row * pitch + column, values.shape[0], stride=pitch), :] = values
+
+    place(turned_ref, 0, 0, jnp.broadcast_to(classes, (grid_rows, angles)))
+    place(turned_ref, 0, 1, gamma)
+    place(turned_ref, cycles, 1, gamma)
     for j in range(owned):
-        turned_ref[(2 + j) * pitch : (2 + j) * pitch + grid_rows, :] = averages_ref[j]
+        place(turned_ref, 0, 2 + j, averages_ref[j])
     for j in range(2 + owned, AUX):
-        turned_ref[j * pitch : j * pitch + grid_rows, :] = jnp.zeros(
-            (grid_rows, angles), jnp.float32
-        )
-
-    def spread_aux(r, carry):
-        got = turned_ref[pl.ds(r, AUX, stride=pitch), :]
-        out_ref[r, pl.ds(count, AUX), :] = got.astype(jnp.bfloat16)
-        return carry
-
-    lax.fori_loop(0, grid_rows, spread_aux, 0, unroll=32)
+        place(turned_ref, 0, j, jnp.zeros((grid_rows, angles), jnp.float32))
+
+    for r in range(grid_rows):
+        got = turned_ref[r * pitch : r * pitch + AUX, :]
+        out_ref[r, count : count + AUX, :] = got.astype(jnp.bfloat16)
     copies[1].wait()
 
     def turn(i, turned):
@@ -122,16 +120,13 @@
             sine = xr * yi + xi * yr
             real = rows_ref[particle, 0].astype(jnp.float32)
             imag = rows_ref[particle, 1].astype(jnp.float32)
-            base = j * pitch
-            turned[base : base + cycles, :] = pltpu.roll(cosine * real - sine * imag, back, 1)
-            turned[base + cycles : base + grid_rows, :] = pltpu.roll(
-                sine * real + cosine * imag, back, 1
-            )
+            place(turned, 0, j, pltpu.roll(cosine * real - sine * imag, back, 1))
+            place(turned, cycles, j, pltpu.roll(sine * real + cosine * imag, back, 1))
 
     def spread(i, turned):
         first = i * BATCH
         for r in range(grid_rows):
-            got = turned[pl.ds(r, BATCH, stride=pitch), :]
+            got = turned[r * pitch : r * pitch + BATCH, :]
             out_ref[r, pl.ds(first, BATCH), :] = got.astype(jnp.bfloat16)
 
     scratches = (turned_ref, other_ref)
@@ -165,8 +160,8 @@
         out_specs=pl.BlockSpec(memory_space=pltpu.VMEM),
         scratch_shapes=[
             pltpu.VMEM((count, 2, cycles, angles), jnp.bfloat16),
-            pltpu.VMEM((BATCH * (grid_rows + PAD), angles), jnp.float32),
-            pltpu.VMEM((BATCH * (grid_rows + PAD), angles), jnp.float32),
+            pltpu.VMEM((grid_rows * (BATCH + PAD), angles), jnp.float32),
+            pltpu.VMEM((grid_rows * (BATCH + PAD), angles), jnp.float32),
             pltpu.VMEM(table.shape, jnp.float32),
             pltpu.SMEM((count,), jnp.int32),
             pltpu.SMEM((count,), jnp.int32),

time: 98 us -> 97.8 us (level)
  no operation moved by 1% of the time
where the time goes in v7:
time: 97.8 us; the launch traced here: 97.3 us
  blocking collectives  82.6 us (84%)
  Pallas kernels  14 us (14%)
    all_to_all x1, blocking collectives, on_device(): lax.all_to_all(sent, everyone, split_axis=0, concat_axis=0, tiled=True)  67.2 us
    all_to_all x1, blocking collectives, on_device(): lax.all_to_all(partial, everyone, split_axis=0, concat_axis=0, tiled=True)  15.4 us
    pallas_call x1, Pallas kernels, class_sums(): pl.pallas_call(classes_kernel, out_shape=jax.ShapeDtypeStruct((devices *...  7.45 us
    pallas_call x1, Pallas kernels, align(): pl.pallas_call(align_kernel, out_shape=jax.ShapeDtypeStruct((grid_rows, c...  5.44 us

profile of v7, /device:TPU:1, one launch (start us, length us, event | category | flops | bytes accessed | tf_op | source)
XLA Modules:
  0.0 97.3 jit_solution(3476689527357863967)
XLA Ops:
  0.6 5.4 %align.1 = bf16[128,136,128]{2,1,0:T(8,128)(2,1)S(1)} custom-call(s32[128]{0:T(128)} %index_hbm.1, s32[128]{0:T(128)} %rot_hbm.1, s32[2,128]{1,0:T(2,128)} %bitcast.16, bf16[256,2,64,128]{3,2,1,0:T(8,128)(2,1)} %stack_hbm.1, f32[2,9,2,64,128]{4,3,2,1,0:T(8,128)} %constant.2.clone.table_hbm, bf16[64,128]{1,0:T(8,128)(2,1)} %bitcast.15, s32[1,128]{1,0:T(1,128)} %bitcast.17, ...), custom_call_target="tpu_custom_call" | custom-call | tf_op jit(solution)/shard_map/align/pallas_call | solution.py:156
  6.1 67.2 %all_to_all.10.received_ref = bf16[128,136,128]{2,1,0:T(8,128)(2,1)S(1)} all-to-all(bf16[128,136,128]{2,1,0:T(8,128)(2,1)S(1)} %align.1), channel_id=1, replica_groups=mesh['dom'=16,'cls'=8] {'dom','cls'}, dimensions={0} | all-to-all | bytes 8912896 | tf_op jit(solution)/shard_map/all_to_all | solution.py:356
  73.2 0.0 copy-start
  73.2 0.0 copy-start.1
  73.3 7.5 %class_sums.1 = bf16[768,128]{1,0:T(8,128)(2,1)S(1)} custom-call(bf16[128,136,128]{2,1,0:T(8,128)(2,1)S(1)} %all_to_all.10.received_ref), custom_call_target="tpu_custom_call" | custom-call | tf_op jit(solution)/shard_map/class_sums/pallas_call | solution.py:276
  80.7 15.4 %all_to_all.11 = bf16[384,2,128]{2,1,0:T(2,128)(2,1)S(1)} all-to-all(bf16[384,2,128]{2,1,0:T(2,128)(2,1)S(1)} %bitcast.12), channel_id=1, replica_groups=mesh['dom'=16,'cls'=8] {'dom','cls'}, dimensions={0} | all-to-all | bytes 393216 | tf_op jit(solution)/shard_map/all_to_all | solution.py:360
  96.1 0.0 copy-done
  96.2 0.0 copy-done.1
  96.2 1.1 %update.1 = (f32[4,128,128]{2,1,0:T(8,128)}, f32[4,128,128]{2,1,0:T(8,128)}, f32[1,128]{1,0:T(1,128)}) custom-call(bf16[768,128]{1,0:T(8,128)(2,1)S(1)} %bitcast.13, f32[4,128,128]{2,1,0:T(8,128)S(1)} %bitcast.11, f32[4,128,128]{2,1,0:T(8,128)S(1)} %bitcast.14), custom_call_target="tpu_custom_call" | custom-call | tf_op jit(solution)/shard_map/update/pallas_call | solution.py:335
Async XLA Ops:
  73.2 22.9 %copy-start = (f32[4,2,64,128]{3,2,1,0:T(8,128)S(1)}, f32[4,2,64,128]{3,2,1,0:T(8,128)}, u32[]{:S(2)}) copy-start(f32[4,2,64,128]{3,2,1,0:T(8,128)} %param.15) | copy-start | bytes 786436
  73.2 22.9 %copy-start.1 = (f32[4,2,64,128]{3,2,1,0:T(8,128)S(1)}, f32[4,2,64,128]{3,2,1,0:T(8,128)}, u32[]{:S(2)}) copy-start(f32[4,2,64,128]{3,2,1,0:T(8,128)} %param.16) | copy-start | bytes 786436

commit v8 on v7

--- a/solution.py
+++ b/solution.py
@@ -11,7 +11,7 @@
 MOMENTUM = 0.9
 RATE = 0.5
 RIDGE = 1.0
-BATCH = 16
+BATCH = 32
 SOURCES = 16
 AUX = 8
 PAD = 8

time: 97.8 us -> 97.3 us (level)
  no operation moved by 1% of the time
where the time goes in v8:
time: 97.3 us; the launch traced here: 97.1 us
  blocking collectives  82.6 us (85%)
  Pallas kernels  13.8 us (14%)
    all_to_all x1, blocking collectives, on_device(): lax.all_to_all(sent, everyone, split_axis=0, concat_axis=0, tiled=True)  67.2 us
    all_to_all x1, blocking collectives, on_device(): lax.all_to_all(partial, everyone, split_axis=0, concat_axis=0, tiled=True)  15.4 us
    pallas_call x1, Pallas kernels, class_sums(): pl.pallas_call(classes_kernel, out_shape=jax.ShapeDtypeStruct((devices *...  7.46 us
    pallas_call x1, Pallas kernels, align(): pl.pallas_call(align_kernel, out_shape=jax.ShapeDtypeStruct((grid_rows, c...  5.19 us

profile of v8, /device:TPU:1, one launch (start us, length us, event | category | flops | bytes accessed | tf_op | source)
XLA Modules:
  0.0 97.1 jit_solution(12345364053390697062)
XLA Ops:
  0.6 5.2 %align.1 = bf16[128,136,128]{2,1,0:T(8,128)(2,1)S(1)} custom-call(s32[128]{0:T(128)} %index_hbm.1, s32[128]{0:T(128)} %rot_hbm.1, s32[2,128]{1,0:T(2,128)} %bitcast.16, bf16[256,2,64,128]{3,2,1,0:T(8,128)(2,1)} %stack_hbm.1, f32[2,9,2,64,128]{4,3,2,1,0:T(8,128)} %constant.2.clone.table_hbm, bf16[64,128]{1,0:T(8,128)(2,1)} %bitcast.15, s32[1,128]{1,0:T(1,128)} %bitcast.17, ...), custom_call_target="tpu_custom_call" | custom-call | tf_op jit(solution)/shard_map/align/pallas_call | solution.py:156
  5.8 67.2 %all_to_all.10.received_ref = bf16[128,136,128]{2,1,0:T(8,128)(2,1)S(1)} all-to-all(bf16[128,136,128]{2,1,0:T(8,128)(2,1)S(1)} %align.1), channel_id=1, replica_groups=mesh['dom'=16,'cls'=8] {'dom','cls'}, dimensions={0} | all-to-all | bytes 8912896 | tf_op jit(solution)/shard_map/all_to_all | solution.py:356
  73.0 0.0 copy-start
  73.0 0.0 copy-start.1
  73.0 7.5 %class_sums.1 = bf16[768,128]{1,0:T(8,128)(2,1)S(1)} custom-call(bf16[128,136,128]{2,1,0:T(8,128)(2,1)S(1)} %all_to_all.10.received_ref), custom_call_target="tpu_custom_call" | custom-call | tf_op jit(solution)/shard_map/class_sums/pallas_call | solution.py:276
  80.5 15.4 %all_to_all.11 = bf16[384,2,128]{2,1,0:T(2,128)(2,1)S(1)} all-to-all(bf16[384,2,128]{2,1,0:T(2,128)(2,1)S(1)} %bitcast.12), channel_id=1, replica_groups=mesh['dom'=16,'cls'=8] {'dom','cls'}, dimensions={0} | all-to-all | bytes 393216 | tf_op jit(solution)/shard_map/all_to_all | solution.py:360
  95.9 0.0 copy-done
  95.9 0.0 copy-done.1
  95.9 1.1 %update.1 = (f32[4,128,128]{2,1,0:T(8,128)}, f32[4,128,128]{2,1,0:T(8,128)}, f32[1,128]{1,0:T(1,128)}) custom-call(bf16[768,128]{1,0:T(8,128)(2,1)S(1)} %bitcast.13, f32[4,128,128]{2,1,0:T(8,128)S(1)} %bitcast.11, f32[4,128,128]{2,1,0:T(8,128)S(1)} %bitcast.14), custom_call_target="tpu_custom_call" | custom-call | tf_op jit(solution)/shard_map/update/pallas_call | solution.py:335
Async XLA Ops:
  73.0 22.9 %copy-start = (f32[4,2,64,128]{3,2,1,0:T(8,128)S(1)}, f32[4,2,64,128]{3,2,1,0:T(8,128)}, u32[]{:S(2)}) copy-start(f32[4,2,64,128]{3,2,1,0:T(8,128)} %param.15) | copy-start | bytes 786436
  73.0 22.9 %copy-start.1 = (f32[4,2,64,128]{3,2,1,0:T(8,128)S(1)}, f32[4,2,64,128]{3,2,1,0:T(8,128)}, u32[]{:S(2)}) copy-start(f32[4,2,64,128]{3,2,1,0:T(8,128)} %param.16) | copy-start | bytes 786436
